TPU v7x, 32 devices: a whole 2x2x4 slice. The times are simulated.
32 devices in a mesh: seq: 16 (over z, y, x), head: 2 (over core).
Axes of the slice: x: 2, y: 2, z: 4, core: 2. Of those that a mesh axis runs over, the one named last changes fastest.
Arguments:
- x_in: bfloat16 [2, 2048, 8192], P(None, 'seq', 'head'), may hold values from -6 to 6
- target: bfloat16 [2, 2048, 8192], P(None, 'seq', 'head'), may hold values from -6 to 6
- b_in: bfloat16 [2, 2048, 1024], P(None, 'seq', 'head'), may hold values from -0.125 to 0.125
- c_in: bfloat16 [2, 2048, 1024], P(None, 'seq', 'head'), may hold values from -0.5 to 0.5
- dt_raw: float32 [2, 128, 2048], P(None, 'head', 'seq'), may hold values from -1 to 2.3
- resets: int32 [2, 2048], P(None, 'seq'), may hold values 0 or 1
- decay_rate: float32 [128], P('head'), may hold values from 0 to 1
- conv_w: float32 [4, 8192], P(None, 'head'), may hold values from -3 to 3
- label: int32 [1], replicated, may hold values from 0 to 1
Outputs:
- loss: float32 [], replicated
- grad_x: bfloat16 [2, 2048, 8192], P(None, 'seq', 'head')
- grad_dt: float32 [2, 128, 2048], P(None, 'head', 'seq')
All inputs are finite; a program needn't handle non-finite values. No bound on the sum of `resets` on one device may be relied on, other than what follows from the above.
Results may differ from a plain program's by a relative error of at most 0.001.
Values may be sent and summed in bfloat16 or wider, within the bound.
A program may use at most 320 MiB of HBM per device.

v0:
```python
import math

import jax
import jax.numpy as jnp
from jax import lax
from jax.sharding import PartitionSpec as P

DSTATE = 128
SPAN = 128


HIGH = lax.Precision.HIGHEST


def shifted(block, axis, distance):
    devices = range(lax.axis_size(axis))
    route = [(i - distance, i) for i in devices if i - distance in devices]
    return lax.ppermute(block, axis, route)


def carried_in(value, axis, join, neutral, backward):
    count, mine = (lax.axis_size(axis), lax.axis_index(axis))
    pieces = jax.tree.map(lambda part: lax.all_gather(part, axis), value)
    if backward:
        pieces = jax.tree.map(lambda part: part[::-1], pieces)
        mine = count - 1 - mine
    subtotal = jax.tree.map(
        lambda part, zero: jnp.full_like(part, 0) + jnp.asarray(zero, part.dtype), value, neutral
    )

    def step(position, subtotal):
        longer = join(subtotal, jax.tree.map(lambda part: part[position], pieces))
        return jax.tree.map(lambda new, old: jnp.where(position < mine, new, old), longer, subtotal)

    return lax.fori_loop(0, count - 1, step, subtotal)


def conv_silu(x_ext, keep_ext, conv_w):
    keep_now = keep_ext[2:][:, None]
    keep_two = keep_now * keep_ext[1:-1][:, None]
    keep_three = keep_two * keep_ext[:-2][:, None]
    pre = conv_w[3] * x_ext[3:] + keep_now * conv_w[2] * x_ext[2:-1]
    pre = pre + keep_two * conv_w[1] * x_ext[1:-2] + keep_three * conv_w[0] * x_ext[:-3]
    return jax.nn.silu(pre)


def ssd_span(state, values, steps, logs, marks, b_rows, c_rows):
    size, heads, width = values.shape
    ratio = heads // b_rows.shape[1]
    running = jnp.cumsum(logs, axis=1)
    seen = jnp.cumsum(marks)
    order = jnp.arange(size)
    valid = (order[:, None] >= order[None, :]) & (seen[:, None] == seen[None, :])
    gap = jnp.where(valid[None], running[:, :, None] - running[:, None, :], 0.0)
    decay = jnp.where(valid[None], jnp.exp(gap), 0.0)
    scores = jnp.einsum("ign,jgn->gij", c_rows, b_rows, precision=HIGH)
    scores = jnp.repeat(scores, ratio, axis=0)
    mixing = decay * scores * steps[:, None, :]
    intra = jnp.einsum("hij,jhp->ihp", mixing, values, precision=HIGH)
    b_heads = jnp.repeat(b_rows, ratio, axis=1)
    c_heads = jnp.repeat(c_rows, ratio, axis=1)
    entry = jnp.exp(running) * (seen == 0.0).astype(running.dtype)[None, :]
    carried = jnp.einsum("ihn,hpn->ihp", c_heads, state, precision=HIGH) * entry.T[:, :, None]
    tail = (
        jnp.exp(running[:, -1:] - running)
        * (seen[-1] == seen).astype(running.dtype)[None, :]
        * steps
    )
    weighted = values * tail.T[:, :, None]
    final = entry[:, -1][:, None, None] * state + jnp.einsum(
        "jhp,jhn->hpn", weighted, b_heads, precision=HIGH
    )
    return (final, intra + carried)


def mixer_rows(state, values, steps, logs, marks, b_rows, c_rows):
    rows, heads, width = values.shape
    count = rows // SPAN

    def blocks(array):
        return array.reshape((count, SPAN) + array.shape[1:])

    def blocks_heads(array):
        return array.reshape(heads, count, SPAN).transpose(1, 0, 2)

    def advance(carry, block):
        return ssd_span(carry, *block)

    final, outs = lax.scan(
        advance,
        state,
        (
            blocks(values),
            blocks_heads(steps),
            blocks_heads(logs),
            blocks(marks),
            blocks(b_rows),
            blocks(c_rows),
        ),
    )
    return (outs.reshape(rows, heads * width), final)


def local_pass(x_ext, raw, state, keep_ext, marks, b_rows, c_rows, conv_w, decay_rate):
    rows = x_ext.shape[0] - 3
    heads = raw.shape[0]
    values = conv_silu(x_ext, keep_ext, conv_w).reshape(rows, heads, -1)
    steps = jax.nn.softplus(raw)
    logs = -steps * decay_rate[:, None]
    return mixer_rows(state, values, steps, logs, marks, b_rows, c_rows)


def forward_join(earlier, later):
    return (earlier[0] * later[0], later[0][:, :, None, None] * earlier[1] + later[1])


def backward_join(earlier, later):
    return (later[0] * earlier[0], later[1] + later[0][:, :, None, None] * earlier[1])


def body(x_in, target, b_in, c_in, dt_raw, resets, decay_rate, conv_w, label):
    rows = x_in.shape[1]
    chans = x_in.shape[2]
    heads = dt_raw.shape[1]
    width = chans // heads
    groups = b_in.shape[2] // DSTATE
    ratio = heads // groups
    marks = resets.astype(jnp.float32)
    edge_rows, edge_marks = shifted(
        (x_in[:, rows - 3 :, :], marks[:, rows - 2 :].astype(jnp.bfloat16)), "seq", 1
    )
    x_ext = jnp.concatenate([edge_rows, x_in], axis=1).astype(jnp.float32)
    keep_ext = 1.0 - jnp.concatenate([edge_marks.astype(jnp.float32), marks], axis=1)
    b_rows = b_in.astype(jnp.float32).reshape(2, rows, groups, DSTATE)
    c_rows = c_in.astype(jnp.float32).reshape(2, rows, groups, DSTATE)
    target_f = target.astype(jnp.float32)
    steps = jax.nn.softplus(dt_raw)
    logs = -steps * decay_rate[None, :, None]
    running = jnp.cumsum(logs, axis=2)
    seen = jnp.cumsum(marks, axis=1)
    clear = (seen == 0.0).astype(jnp.float32)
    through = jnp.exp(running[:, :, -1]) * clear[:, -1:]
    reach = (
        jnp.exp(running[:, :, -1:] - running)
        * (seen[:, -1:] == seen).astype(jnp.float32)[:, None, :]
        * steps
    )
    values = jax.vmap(conv_silu, in_axes=(0, 0, None))(x_ext, keep_ext, conv_w).reshape(
        2, rows, heads, width
    )
    b_heads = jnp.repeat(b_rows, ratio, axis=2)
    c_heads = jnp.repeat(c_rows, ratio, axis=2)
    alone = jnp.einsum("bhr,brhp,brhn->bhpn", reach, values, b_heads, precision=HIGH)
    neutral = (jnp.ones_like(through), jnp.zeros_like(alone))
    carried, start = carried_in((through, alone), "seq", forward_join, neutral, False)

    def single(x_one, raw_one, state_one, keep_one, marks_one, b_one, c_one):
        return local_pass(
            x_one, raw_one, state_one, keep_one, marks_one, b_one, c_one, conv_w, decay_rate
        )

    def paired(x_all, raw_all, state_all):
        return jax.vmap(single)(x_all, raw_all, state_all, keep_ext, marks, b_rows, c_rows)

    (outs, finals), pullback = jax.vjp(paired, x_ext, dt_raw, start)
    partial_sums = jnp.sum(outs * target_f, axis=(1, 2))
    totals = lax.psum(partial_sums, ("seq", "head"))
    count = rows * lax.axis_size("seq") * chans * lax.axis_size("head")
    scores = totals / math.sqrt(count)
    sign = jnp.where(jnp.arange(2) == label[0], 1.0, -1.0).astype(jnp.float32)
    margin = jnp.sum(sign * scores)
    loss = jax.nn.softplus(-margin)
    factor = -jax.nn.sigmoid(-margin) * sign
    entry = jnp.exp(running) * clear[:, None, :]
    seed = jnp.einsum(
        "bhr,brhp,brhn->bhpn",
        entry,
        target_f.reshape(2, rows, heads, width),
        c_heads,
        precision=HIGH,
    )
    passed, later_grad = carried_in((through, seed), "seq", backward_join, neutral, True)
    grad_ext, grad_raw, grad_start = pullback((target_f, later_grad))
    grad_ext = factor[:, None, None] * grad_ext
    grad_raw = factor[:, None, None] * grad_raw
    back_rows = shifted(grad_ext[:, :3, :], "seq", -1)
    inner = grad_ext[:, 3:, :]
    grad_x = jnp.concatenate([inner[:, : rows - 3, :], inner[:, rows - 3 :, :] + back_rows], axis=1)
    return (loss, grad_x.astype(jnp.bfloat16), grad_raw)


def solution(mesh):
    in_specs = (
        P(None, "seq", "head"),
        P(None, "seq", "head"),
        P(None, "seq", "head"),
        P(None, "seq", "head"),
        P(None, "head", "seq"),
        P(None, "seq"),
        P("head"),
        P(None, "head"),
        P(),
    )
    out_specs = (P(), P(None, "seq", "head"), P(None, "head", "seq"))
    return jax.shard_map(body, mesh=mesh, in_specs=in_specs, out_specs=out_specs, check_vma=False)
```

profile of v0, /device:TPU:0, one launch (start us, length us, event | category | flops | bytes accessed | tf_op | source)
XLA Modules:
  0.0 1789.6 jit_solution(4049874946242295587)
XLA Ops:
  20.5 9.4 fusion.19
  41.2 38.1 %all_gather.18 = f32[16,2,64]{2,1,0:T(2,128)S(1)} all-gather(f32[1,2,64]{2,1,0:T(2,128)S(1)} %bitcast_multiply_fusion.8), channel_id=1, replica_groups=mesh['seq'=16,'head'=2] {'seq'}, dimensions={0}, use_global_device_ids=true | all-gather | bytes 8704 | tf_op jit(solution)/shard_map/all_gather | solution.py:23
  89.7 611.3 %all-gather.7.cloned.1.call-done = f32[32,64,64,128]{3,2,1,0:T(8,128)} async-done(((f32[2,64,64,128]{3,2,1,0:T(8,128)}), f32[32,64,64,128]{3,2,1,0:T(8,128)}) %all-gather.7.cloned.1.call-update) | async-done | bytes 67108880 | tf_op jit(solution)/shard_map/all_gather | solution.py:23
  701.0 43.5 %rev.6 = f32[16,2,64,64,128]{4,3,2,1,0:T(8,128)} reverse(f32[16,2,64,64,128]{4,3,2,1,0:T(8,128)} %bitcast.16), dimensions={0} | reverse | bytes 134217728 | tf_op jit(solution)/shard_map/rev | solution.py:25
  744.6 98.6 %while.21 = (s32[]{:T(128)}, f32[2,64,64,128]{3,2,1,0:T(8,128)}, s32[]{:T(128)}, f32[16,2,64,64,128]{4,3,2,1,0:T(8,128)}, f32[16,2,64]{2,1,0:T(2,128)}, /*index=5*/s32[]{:T(128)}, s32[]{:T(128)}) while((s32[]{:T(128)}, f32[2,64,64,128]{3,2,1,0:T(8,128)}, s32[]{:T(128)}, f32[16,2,64,64,128]{4,3,2,1,0:T(8,128)}, ...), condition=%wide.region_8.9_spmd.clone, body=%wide.region_7.8_spmd.clone.sunk | while | flops 4194308 | bytes 12584553 | solution.py:35
  750.6 6.0 fusion.77
  757.3 6.0 fusion.77
  763.9 6.0 fusion.77
  770.6 6.0 fusion.77
  777.2 6.0 fusion.77
  783.8 6.0 fusion.77
  790.5 6.0 fusion.77
  797.1 6.0 fusion.77
  803.8 6.0 fusion.77
  810.4 6.0 fusion.77
  817.1 6.0 fusion.77
  823.7 6.0 fusion.77
  830.4 6.0 fusion.77
  837.0 6.0 fusion.77
  845.8 16.7 fusion.61
  864.7 8.7 bitcast_add_fusion.2
  873.4 5.6 copy.43
  879.0 13.6 multiply_multiply_fusion
  895.7 5.6 copy.38
  901.3 11.8 fusion.22
  918.3 6.8 fusion.16
  925.4 15.4 fusion.39
  946.0 633.6 %all-gather.5.cloned.1.call-done = f32[32,64,64,128]{3,2,1,0:T(8,128)} async-done(((f32[2,64,64,128]{3,2,1,0:T(8,128)}), f32[32,64,64,128]{3,2,1,0:T(8,128)}) %all-gather.5.cloned.1.call-update) | async-done | bytes 67108880 | tf_op jit(solution)/shard_map/all_gather | solution.py:23
  1579.6 88.9 %while.20 = (s32[]{:T(128)}, f32[2,64,64,128]{3,2,1,0:T(8,128)}, s32[]{:T(128)}, f32[16,2,64]{2,1,0:T(2,128)S(1)}, f32[16,2,64,64,128]{4,3,2,1,0:T(8,128)}, /*index=5*/s32[]{:T(128)}, s32[]{:T(128)}) while((s32[]{:T(128)}, f32[2,64,64,128]{3,2,1,0:T(8,128)}, s32[]{:T(128)}, f32[16,2,64]{2,1,0:T(2,128)S(1)}, ...), condition=%wide.region_3.4_spmd.clone, body=%wide.region_2.3_spmd.clone.sunk | while | flops 4194308 | bytes 12584553 | solution.py:35
  1584.3 6.0 fusion.76
  1590.3 6.0 fusion.76
  1596.3 6.0 fusion.76
  1602.4 6.0 fusion.76
  1608.4 6.0 fusion.76
  1614.4 6.0 fusion.76
  1620.4 6.0 fusion.76
  1626.4 6.0 fusion.76
  1632.4 6.0 fusion.76
  1638.4 6.0 fusion.76
  1644.4 6.0 fusion.76
  1650.4 6.0 fusion.76
  1656.4 6.0 fusion.76
  1662.5 6.0 fusion.76
  1672.7 20.3 %fusion.18 = (f32[2,128,64]{1,2,0:T(8,128)S(1)}, f32[2,64,64,128]{3,2,1,0:T(8,128)S(1)}) fusion(f32[2,128,4096]{1,2,0:T(8,128)} %copy.47, f32[2,64,64,128]{3,2,1,0:T(8,128)} %get-tuple-element.457, f32[2,128,64,128]{3,1,2,0:T(8,128)} %bitcast.138), kind=kOutput, calls=%fused_computation.41 | convolution fusion | flops 1612693504 | bytes 21037056 | tf_op jit(solution)/shard_map/jvp(vmap())/while/body/eval_jaxpr/ihn,hpn->ihp/dot_general | solution.py:63
  1692.9 20.9 %fusion.17 = f32[2,128,64,64]{1,3,2,0:T(8,128)} fusion(f32[2,64,64,128]{3,2,1,0:T(8,128)S(1)} %get-tuple-element.542, f32[2,128,64]{1,2,0:T(8,128)S(1)} %copy-done.14, f32[2,128,64,64]{1,3,2,0:T(8,128)S(1)} %bitcast.143, f32[2,64,128]{2,1,0:T(8,128)S(1)} %copy-done.15, f32[2,64,128,128]{3,2,1,0:T(8,128)} %bitcast.146, ...), kind=kOutput, calls=%fused_computation.40 | convolution fusion | flops 1623195648 | bytes 21200896 | tf_op jit(solution)/shard_map/jvp(vmap())/while/body/eval_jaxpr/hij,jhp->ihp/dot_general | solution.py:59
  1713.9 5.8 copy.41
  1725.2 38.4 %psum.7 = f32[2]{0:T(128)S(1)} all-reduce(f32[2]{0:T(128)S(1)} %multiply_reduce_fusion.1), channel_id=1, replica_groups=mesh['seq'=16,'head'=2] {'seq','head'}, use_global_device_ids=true, to_apply=%region_5.6 | all-reduce | flops 2 | bytes 16 | tf_op jit(solution)/shard_map/psum | solution.py:167
  1764.9 6.8 add_multiply_fusion
  (144 shorter events, 91.1 us)
Async XLA Ops:
  7.2 8.1 copy-start.10
  7.2 693.8 %all-gather.7.cloned.1.call-start = ((), (), s32[]{:S(2)}) async-start(), calls=%async_computation.1 | async-start | bytes 71303168 | tf_op jit(solution)/shard_map/all_gather | solution.py:23
  9.5 7.7 copy-start.18
  10.2 0.6 copy-start.25
  10.8 6.4 copy-start.22
  11.1 6.2 copy-start.20
  11.1 29.9 %copy-start.23 = (f32[2,128]{1,0:T(2,128)}, f32[2,128]{1,0:T(2,128)S(1)}, u32[]{:S(2)}) copy-start(f32[2,128]{1,0:T(2,128)S(1)} %get-tuple-element.538) | copy-start | bytes 3076
  15.3 848.4 %copy-start.9 = (bf16[2,128,4096]{1,2,0:T(8,128)(2,1)}, bf16[2,128,4096]{1,2,0:T(8,128)(2,1)S(1)}, u32[]{:S(2)}) copy-start(bf16[2,128,4096]{1,2,0:T(8,128)(2,1)S(1)} %copy.42) | copy-start | bytes 6291460
  16.2 1.1 copy-start.13
  17.3 3.2 copy-start.1
  29.9 50.1 %copy-start.12 = (bf16[2,128,512]{2,1,0:T(8,128)(2,1)S(1)}, bf16[2,128,512]{2,1,0:T(8,128)(2,1)}, u32[]{:S(2)}) copy-start(bf16[2,128,512]{2,1,0:T(8,128)(2,1)} %param.15) | copy-start | bytes 786436
  29.9 51.7 %copy-start.11 = (bf16[2,128,512]{2,1,0:T(8,128)(2,1)S(1)}, bf16[2,128,512]{2,1,0:T(8,128)(2,1)}, u32[]{:S(2)}) copy-start(bf16[2,128,512]{2,1,0:T(8,128)(2,1)} %param.16) | copy-start | bytes 786436
  29.9 1549.7 %all-gather.5.cloned.1.call-start = ((), (), s32[]{:S(2)}) async-start(), calls=%async_computation | async-start | bytes 71303168 | tf_op jit(solution)/shard_map/all_gather | solution.py:23
  30.5 53.3 %collective-permute-start.1 = (bf16[2,2]{1,0:T(2,128)(2,1)}, bf16[2,2]{1,0:T(2,128)(2,1)}, u32[]{:S(2)}, u32[]{:S(2)}) collective-permute-start(bf16[2,2]{1,0:T(2,128)(2,1)} %slice.92), channel_id=1, source_target_pairs={{0,2},{2,4},{4,6},{6,8},{8,10},{10,12},{12,14},{14,16},{16,18},{18... | collective-permute-start | bytes 32 | tf_op jit(solution)/shard_map/ppermute | solution.py:18
  37.5 47.8 %collective-permute-start = (bf16[2,3,4096]{2,1,0:T(4,128)(2,1)}, bf16[2,3,4096]{2,1,0:T(4,128)(2,1)}, u32[]{:S(2)}, u32[]{:S(2)}) collective-permute-start(bf16[2,3,4096]{2,1,0:T(4,128)(2,1)} %slice.90), channel_id=1, source_target_pairs={{0,2},{2,4},{4,6},{6,8},{8,10},{10,12},{12,14},{14,16},{16,18},{18... | collective-permute-start | bytes 147464 | tf_op jit(solution)/shard_map/ppermute | solution.py:18
  843.2 2.6 copy-start
  844.2 18.3 %copy-start.2 = (f32[2,128,4,16,128]{4,1,3,2,0:T(8,128)}, f32[2,128,4,16,128]{4,1,3,2,0:T(8,128)S(1)}, u32[]{:S(2)}) copy-start(f32[2,128,4,16,128]{4,1,3,2,0:T(8,128)S(1)} %broadcast_in_dim.197) | copy-start | bytes 25165828
  862.5 1.9 copy-start.7
  862.5 2.1 copy-start.15
  862.6 2.1 copy-start.16
  862.6 2.1 copy-start.17
  863.7 9.8 copy-start.4
  913.1 1.6 copy-start.5
  918.3 6.8 copy-start.19
  918.3 6.8 copy-start.21
  925.4 15.4 copy-start.6
  1672.6 20.3 %copy-start.3 = (f32[2,128,4096]{1,2,0:T(8,128)S(1)}, f32[2,128,4096]{1,2,0:T(8,128)}, u32[]{:S(2)}) copy-start(f32[2,128,4096]{1,2,0:T(8,128)} %copy.38) | copy-start | bytes 12582916
  1672.7 20.3 %copy-start.14 = (f32[2,128,64]{1,2,0:T(8,128)S(1)}, f32[2,128,64]{1,2,0:T(8,128)}, u32[]{:S(2)}) copy-start(f32[2,128,64]{1,2,0:T(8,128)} %copy-done.13) | copy-start | bytes 196612
  1719.7 2.8 copy-start.24
  1764.9 8.1 copy-start.26
  1771.7 2.1 copy-start.8
  1771.8 7.1 collective-permute-start.2
Sparse Core Ops, SparseCore 0:
  30.0 670.9 all-gather.6
  913.2 666.3 all-gather.4
where the time goes:
time: 1800 us; the launch traced here: 1790 us
  waiting for transfers between devices  1250 us (69%)
  other arithmetic  238 us (13%)
  matrix products  104 us (6%)
  local copies, waits for them, and re-layouts  93.6 us (5%)
  blocking collectives  76.4 us (4%)
  between operations  18 us (1%)
    all_gather x2, waiting for transfers between devices, carried_in(): pieces = jax.tree.map(lambda part: lax.all_gather(part, axis), value)  1240 us
    select_n x30, other arithmetic, step(): jnp.where(position < mine, new, old)  177 us
    dot_general x3, matrix products, ssd_span(): intra = jnp.einsum('hij,jhp->ihp', mixing, values, precision=HIGH)  45 us
    rev x2, local copies, waits for them, and re-layouts, carried_in(): pieces = jax.tree.map(lambda part: part[::-1], pieces)  44.2 us
    psum x1, blocking collectives, body(): totals = lax.psum(partial_sums, ('seq', 'head'))  38.4 us
    all_gather x1, blocking collectives, carried_in(): pieces = jax.tree.map(lambda part: lax.all_gather(part, axis), value)  38.1 us
  transfers between devices with their start and end apart: 5, of which 3 were waited for; matrix products, arithmetic and copies ran while one was open for 2% of the time, Pallas kernels for 0%

commit v1 on v0

v1 whole, which is shorter than its diff:
```python
import functools
import math

import jax
import jax.numpy as jnp
from jax import lax
from jax.experimental import pallas as pl
from jax.experimental.pallas import tpu as pltpu
from jax.sharding import Mesh
from jax.sharding import PartitionSpec as P

DSTATE = 128
SPAN = 128
LANES = 128
TAPS = 4
HALO = 16
FAR = -1e30
HIGH = lax.Precision.HIGHEST
F32 = jnp.float32
BF16 = jnp.bfloat16


def split(value):
    high = value.astype(BF16)
    low = (value - high.astype(F32)).astype(BF16)
    return high, low


def mm(left, right):
    return lax.dot_general(left, right, (((1,), (0,)), ((), ())), preferred_element_type=F32)


def mm_exact_left(left, right):
    high, low = split(right)
    return mm(left, high) + mm(left, low)


def mm_exact_right(left, right):
    high, low = split(left)
    return mm(high, right) + mm(low, right)


def spread_matrix(offset, chans, width):
    row = lax.broadcasted_iota(jnp.int32, (LANES, chans), 0)
    head = lax.broadcasted_iota(jnp.int32, (LANES, chans), 1) // width
    return jnp.where(row == head + offset, 1.0, 0.0).astype(BF16)


def gather_matrix(chans, width):
    head = lax.broadcasted_iota(jnp.int32, (chans, LANES), 0) // width
    col = lax.broadcasted_iota(jnp.int32, (chans, LANES), 1)
    return jnp.where(col == head, 1.0, 0.0).astype(BF16)


def conv_of(x_ref, xe_scr, w_ref, tok, lane, first):
    xe_scr[...] = x_ref[pl.ds(first, SPAN + HALO), :].astype(F32)
    pre = w_ref[3:4, :] * xe_scr[pl.ds(HALO, SPAN), :]
    for back in range(1, TAPS):
        scale = tok[:, lane + back - 1 : lane + back] * w_ref[3 - back : 4 - back, :]
        pre = pre + scale * xe_scr[pl.ds(HALO - back, SPAN), :]
    return pre


def ends_kernel(heads, count, x_ref, t_ref, bt_ref, ct_ref, tok_ref, w_ref, alone_ref, seed_ref, xe_scr):
    chans = x_ref.shape[1]
    width = chans // heads
    spread_entry = spread_matrix(heads, chans, width)
    spread_tail = spread_matrix(3 * heads, chans, width)
    alone_ref[...] = jnp.zeros_like(alone_ref)
    seed_ref[...] = jnp.zeros_like(seed_ref)

    def forward(k, carry):
        first = pl.multiple_of(k * SPAN, SPAN)
        tok = tok_ref[pl.ds(first, SPAN), :]
        values = jax.nn.silu(conv_of(x_ref, xe_scr, w_ref, tok, 5 * heads, first))
        weighted = values * mm_exact_right(tok, spread_tail)
        through = mm_exact_right(tok[SPAN - 8 :, :], spread_entry)[7:8, :]
        added = mm_exact_left(bt_ref[:, pl.ds(first, SPAN)], weighted)
        alone_ref[...] = through * alone_ref[...] + added
        return carry

    lax.fori_loop(0, count, forward, 0)

    def backward(step, carry):
        first = pl.multiple_of((count - 1 - step) * SPAN, SPAN)
        tok = tok_ref[pl.ds(first, SPAN), :]
        entry = mm_exact_right(tok, spread_entry)
        weighted = entry * t_ref[pl.ds(first, SPAN), :].astype(F32)
        added = mm_exact_left(ct_ref[:, pl.ds(first, SPAN)], weighted)
        seed_ref[...] = entry[SPAN - 1 : SPAN, :] * seed_ref[...] + added
        return carry

    lax.fori_loop(0, count, backward, 0)


def main_kernel(
    heads, count, x_ref, t_ref, b_ref, c_ref, bt_ref, ct_ref, tok_ref, row_ref, w_ref, rate_ref,
    start_ref, later_ref, grad_ref, ddt_ref, score_ref, xe_scr, s_scr, g_scr, v_scr, y_scr, d_scr, cv_scr,
):
    chans = x_ref.shape[1]
    width = chans // heads
    per = LANES // width
    spread_steps = spread_matrix(0, chans, width)
    spread_entry = spread_matrix(heads, chans, width)
    spread_reach = spread_matrix(2 * heads, chans, width)
    spread_tail = spread_matrix(3 * heads, chans, width)
    gather = gather_matrix(chans, width)
    s_scr[0] = start_ref[...]
    g_scr[...] = later_ref[...]
    score_ref[...] = jnp.zeros_like(score_ref)
    cv_scr[...] = jnp.zeros_like(cv_scr)
    total = count * SPAN
    grad_ref[pl.ds(total, HALO), :] = jnp.zeros((HALO, chans), F32)

    def forward(k, carry):
        first = pl.multiple_of(k * SPAN, SPAN)
        tok = tok_ref[pl.ds(first, SPAN), :]
        pre = conv_of(x_ref, xe_scr, w_ref, tok, 5 * heads, first)
        v_scr[pl.ds(first, SPAN), :] = pre
        weighted = jax.nn.silu(pre) * mm_exact_right(tok, spread_tail)
        through = mm_exact_right(tok[SPAN - 8 :, :], spread_entry)[7:8, :]
        added = mm_exact_left(bt_ref[:, pl.ds(first, SPAN)], weighted)
        s_scr[k + 1] = through * s_scr[k] + added
        return carry

    lax.fori_loop(0, count, forward, 0)

    def backward(step, carry):
        k = count - 1 - step
        first = pl.multiple_of(k * SPAN, SPAN)
        here = pl.ds(first, SPAN)
        tok = tok_ref[here, :]
        pre = v_scr[here, :]
        sig = jax.nn.sigmoid(pre)
        values = pre * sig
        slope = sig * (1.0 + pre * (1.0 - sig))
        target = t_ref[here, :]
        b_rows = b_ref[here, :]
        c_rows = c_ref[here, :]
        bt = bt_ref[:, here]
        ct = ct_ref[:, here]
        steps = mm_exact_right(tok, spread_steps)
        entry = mm_exact_right(tok, spread_entry)
        reach = mm_exact_right(tok, spread_reach)
        y_scr[...] = entry * mm_exact_left(c_rows, s_scr[k])
        d_scr[...] = reach * mm_exact_left(b_rows, g_scr[...])
        u_high, u_low = split(steps * values)
        scores = mm(c_rows, bt)
        scores_t = mm(b_rows, ct)
        seen_col = tok[:, 5 * heads + 3 : 5 * heads + 4]
        seen_row = row_ref[5 * heads + 3 : 5 * heads + 4, here]
        order_row = lax.broadcasted_iota(jnp.int32, (SPAN, SPAN), 0)
        order_col = lax.broadcasted_iota(jnp.int32, (SPAN, SPAN), 1)
        same = seen_col == seen_row
        valid = same & (order_row >= order_col)
        valid_t = same & (order_row <= order_col)
        lane = lax.broadcasted_iota(jnp.int32, (SPAN, LANES), 1) // width
        for unit in range(heads // per):
            cols = slice(unit * LANES, (unit + 1) * LANES)
            t_unit = target[:, cols]
            both = jnp.concatenate([u_high[:, cols], u_low[:, cols]], axis=1)
            y_unit = jnp.zeros((SPAN, LANES), F32)
            d_unit = jnp.zeros((SPAN, LANES), F32)
            for part in range(per):
                h = 4 * heads + unit * per + part
                r_col = tok[:, h : h + 1]
                r_row = row_ref[h : h + 1, here]
                gap = r_col - r_row
                mix = jnp.exp(jnp.where(valid, gap, FAR)) * scores
                mix_t = jnp.exp(jnp.where(valid_t, -gap, FAR)) * scores_t
                m_high, m_low = split(mix)
                n_high, n_low = split(mix_t)
                wide = mm(m_high, both)
                y_part = wide[:, :LANES] + wide[:, LANES:] + mm(m_low, both[:, :LANES])
                d_part = mm(n_high, t_unit) + mm(n_low, t_unit)
                y_unit = jnp.where(lane == part, y_part, y_unit)
                d_unit = jnp.where(lane == part, d_part, d_unit)
            y_scr[:, cols] += y_unit
            d_scr[:, cols] += d_unit
        target_f = target.astype(F32)
        read = y_scr[...] * target_f
        score_ref[...] += jnp.sum(read.reshape(SPAN // 8, 8, chans), axis=0)
        du = d_scr[...]
        by_read = mm_exact_right(read, gather)
        by_step = mm_exact_right(values * du, gather)
        cross = jnp.sum((s_scr[k + 1] * g_scr[...]).reshape(DSTATE // 8, 8, chans), axis=0)
        crossed = jnp.sum(mm_exact_right(cross, gather), axis=0, keepdims=True)
        upper = jnp.where(order_row <= order_col, 1.0, 0.0).astype(BF16)
        d_log = mm_exact_left(upper, by_read - tok * by_step) + crossed
        ddt_ref[here, :] = by_step - rate_ref[...] * d_log
        d_pre = steps * du * slope
        cv_scr[0, pl.ds(HALO, SPAN), :] = w_ref[3:4, :] * d_pre
        for back in range(1, TAPS):
            scale = tok[:, 5 * heads + back - 1 : 5 * heads + back] * w_ref[3 - back : 4 - back, :]
            cv_scr[back, pl.ds(HALO, SPAN), :] = scale * d_pre
        top = cv_scr[0, pl.ds(0, SPAN), :]
        end = cv_scr[0, pl.ds(SPAN, HALO), :]
        for back in range(1, TAPS):
            top = top + cv_scr[back, pl.ds(back, SPAN), :]
            end = end + cv_scr[back, pl.ds(SPAN + back, HALO), :]
        grad_ref[here, :] = top
        tail = pl.ds(pl.multiple_of(first + SPAN, SPAN), HALO)
        grad_ref[tail, :] += end
        weighted = entry * target_f
        g_scr[...] = entry[SPAN - 1 : SPAN, :] * g_scr[...] + mm_exact_left(ct, weighted)
        return carry

    lax.fori_loop(0, count, backward, 0)


def per_pair(shape):
    return pl.BlockSpec((None,) + tuple(shape), lambda b: (b,) + (0,) * len(shape))


def whole(shape):
    return pl.BlockSpec(tuple(shape), lambda b: (0,) * len(shape))


def ends(x_ext, target, b_t, c_t, tok, taps, heads):
    pairs, rows, chans = target.shape
    out = jax.ShapeDtypeStruct((pairs, DSTATE, chans), F32)
    return pl.pallas_call(
        functools.partial(ends_kernel, heads, rows // SPAN),
        grid=(pairs,),
        out_shape=(out, out),
        in_specs=[per_pair(a.shape[1:]) for a in (x_ext, target, b_t, c_t, tok)] + [whole(taps.shape)],
        out_specs=(per_pair(out.shape[1:]),) * 2,
        scratch_shapes=[pltpu.VMEM((SPAN + HALO, chans), F32)],
        name="ends",
    )(x_ext, target, b_t, c_t, tok, taps)


def main(x_ext, target, b_rows, c_rows, b_t, c_t, tok, table, taps, rate, start, later, heads):
    pairs, rows, chans = target.shape
    count = rows // SPAN
    outs = (
        jax.ShapeDtypeStruct((pairs, rows + HALO, chans), F32),
        jax.ShapeDtypeStruct((pairs, rows, LANES), F32),
        jax.ShapeDtypeStruct((pairs, 8, chans), F32),
    )
    return pl.pallas_call(
        functools.partial(main_kernel, heads, count),
        grid=(pairs,),
        out_shape=outs,
        in_specs=[per_pair(a.shape[1:]) for a in (x_ext, target, b_rows, c_rows, b_t, c_t, tok, table)]
        + [whole(taps.shape), whole(rate.shape)]
        + [per_pair(start.shape[1:])] * 2,
        out_specs=tuple(per_pair(o.shape[1:]) for o in outs),
        scratch_shapes=[
            pltpu.VMEM((SPAN + HALO, chans), F32),
            pltpu.VMEM((count + 1, DSTATE, chans), F32),
            pltpu.VMEM((DSTATE, chans), F32),
            pltpu.VMEM((rows, chans), F32),
            pltpu.VMEM((SPAN, chans), F32),
            pltpu.VMEM((SPAN, chans), F32),
            pltpu.VMEM((TAPS, SPAN + 2 * HALO, chans), F32),
        ],
        name="main",
    )(x_ext, target, b_rows, c_rows, b_t, c_t, tok, table, taps, rate, start, later)


def chain(through, alone, axis, backward):
    count = lax.axis_size(axis)
    mine = lax.axis_index(axis)
    if backward:
        mine = count - 1 - mine
    carried = jnp.zeros_like(alone)

    def hop(step, carried):
        leaving = through * carried + alone
        if backward:
            route = [(i, i - 1) for i in range(1, count)]
        else:
            route = [(i, i + 1) for i in range(count - 1)]
        arrived = lax.ppermute(leaving, axis, route)
        return jnp.where(mine == step, arrived, carried)

    if count <= 8:
        for step in range(1, count):
            leaving = through * carried + alone
            source, goal = (count - step, count - step - 1) if backward else (step - 1, step)
            arrived = lax.ppermute(leaving, axis, [(source, goal)])
            carried = jnp.where(mine == step, arrived, carried)
        return carried
    return lax.fori_loop(1, count, hop, carried)


def body(outer, inner, x_in, target, b_in, c_in, dt_raw, resets, decay_rate, conv_w, label):
    rows = x_in.shape[1]
    all_heads = dt_raw.shape[1]
    width = x_in.shape[2] // all_heads
    parts = lax.axis_size(inner)
    heads = all_heads // parts
    chans = heads * width
    states = b_in.shape[2] // parts
    tokens = rows * parts
    count = tokens // SPAN
    mine = lax.axis_index(inner)

    def exchange(array):
        if parts == 1:
            return array
        return lax.all_to_all(array, inner, 0, 0, tiled=True)

    def cut(array):
        return array.reshape(2, rows, parts, -1)

    packed = jnp.concatenate([cut(x_in), cut(target), cut(b_in), cut(c_in)], axis=3)
    packed = exchange(packed.transpose(2, 0, 1, 3))
    packed = packed.transpose(1, 0, 2, 3).reshape(2, tokens, -1)
    x_all = packed[:, :, :chans]
    t_all = packed[:, :, chans : 2 * chans]
    b_all = packed[:, :, 2 * chans : 2 * chans + states]
    c_all = packed[:, :, 2 * chans + states :]
    marks = resets.astype(F32)
    small = jnp.concatenate(
        [dt_raw.reshape(2, parts, heads, rows), jnp.broadcast_to(marks[:, None, None, :], (2, parts, 1, rows))], axis=2
    )
    small = exchange(small.transpose(1, 0, 2, 3))
    small = small.transpose(1, 2, 0, 3).reshape(2, heads + 1, tokens)
    raw = small[:, :heads]
    marks = small[:, heads]
    planes = lax.axis_size(outer)
    ahead = [(i, i + 1) for i in range(planes - 1)]
    edge_rows = lax.ppermute(x_all[:, tokens - HALO :], outer, ahead)
    edge_marks = lax.ppermute(marks[:, tokens - 2 :], outer, ahead)
    x_ext = jnp.concatenate([edge_rows, x_all], axis=1)
    keep = 1.0 - jnp.concatenate([edge_marks, marks], axis=1)
    keep_one = keep[:, 2:]
    keep_two = keep_one * keep[:, 1:-1]
    keep_three = keep_two * keep[:, :-2]
    rate = lax.dynamic_slice(decay_rate, (mine * heads,), (heads,))
    taps = lax.dynamic_slice(conv_w, (0, mine * chans), (TAPS, chans))
    steps = jax.nn.softplus(raw)
    logs = -steps * rate[None, :, None]
    upto = jnp.tril(jnp.ones((SPAN, SPAN), F32))
    both = jnp.concatenate([logs, marks[:, None]], axis=1).reshape(2, heads + 1, count, SPAN)
    sums = jnp.einsum("bhkj,ij->bhki", both, upto, precision=HIGH)
    running = sums[:, :heads]
    seen = jnp.round(sums[:, heads:])
    entry = jnp.exp(running) * (seen == 0.0).astype(F32)
    reach = jnp.exp(running[..., -1:] - running) * (seen[..., -1:] == seen).astype(F32)
    through = jnp.prod(entry[..., -1], axis=2)

    def flat(array):
        return array.reshape(2, -1, tokens)

    used = 5 * heads + 4
    table = jnp.concatenate(
        [
            steps,
            flat(entry),
            flat(reach),
            flat(reach) * steps,
            flat(running),
            keep_one[:, None],
            keep_two[:, None],
            keep_three[:, None],
            flat(seen),
            jnp.zeros((2, LANES - used, tokens), F32),
        ],
        axis=1,
    )
    tok = table.transpose(0, 2, 1)
    b_t = b_all.transpose(0, 2, 1)
    c_t = c_all.transpose(0, 2, 1)
    alone, seed = ends(x_ext, t_all, b_t, c_t, tok, taps, heads)
    wide = jnp.repeat(through, width, axis=1)[:, None, :]
    start = chain(wide, alone, outer, False)
    later = chain(wide, seed, outer, True)
    rate_row = jnp.pad(rate, (0, LANES - heads))[None]
    grad, ddt, score = main(x_ext, t_all, b_all, c_all, b_t, c_t, tok, table, taps, rate_row, start, later, heads)
    totals = lax.psum(jnp.sum(score, axis=(1, 2)), (outer, inner, "head"))
    size = tokens * planes * x_in.shape[2] * lax.axis_size("head")
    scores = totals / math.sqrt(size)
    sign = jnp.where(jnp.arange(2) == label[0], 1.0, -1.0).astype(F32)
    margin = jnp.sum(sign * scores)
    loss = jax.nn.softplus(-margin)
    factor = -jax.nn.sigmoid(-margin) * sign
    back_rows = lax.ppermute(grad[:, :HALO], outer, [(i + 1, i) for i in range(planes - 1)])
    grad = grad[:, HALO:]
    grad = jnp.concatenate([grad[:, : tokens - HALO], grad[:, tokens - HALO :] + back_rows], axis=1)
    grad = (factor[:, None, None] * grad).astype(BF16)
    grad = exchange(grad.reshape(2, parts, rows, chans).transpose(1, 0, 2, 3))
    grad = grad.transpose(1, 2, 0, 3).reshape(2, rows, parts * chans)
    grad_raw = factor[:, None, None] * jax.nn.sigmoid(raw) * ddt[:, :, :heads].transpose(0, 2, 1)
    grad_raw = exchange(grad_raw.reshape(2, heads, parts, rows).transpose(2, 0, 1, 3))
    grad_raw = grad_raw.transpose(1, 0, 2, 3).reshape(2, all_heads, rows)
    return (loss, grad, grad_raw)


def solution(mesh):
    def program(*arrays):
        ways, across = mesh.shape["seq"], mesh.shape["head"]
        groups = arrays[2].shape[2] // DSTATE // across
        parts = math.gcd(groups, ways)
        devices = mesh.devices.reshape(ways // parts, parts, across)
        finer = Mesh(devices, ("outer", "inner", "head"))
        seq = ("outer", "inner")
        in_specs = (
            P(None, seq, "head"),
            P(None, seq, "head"),
            P(None, seq, "head"),
            P(None, seq, "head"),
            P(None, "head", seq),
            P(None, seq),
            P("head"),
            P(None, "head"),
            P(),
        )
        out_specs = (P(), P(None, seq, "head"), P(None, "head", seq))
        inner = functools.partial(body, "outer", "inner")
        mapped = jax.shard_map(inner, mesh=finer, in_specs=in_specs, out_specs=out_specs, check_vma=False)
        return mapped(*arrays)

    return program
```

time: 1800 us -> 338 us (0.19)
  waiting for transfers between devices: 1250 us -> 135 us
  other arithmetic: 238 us -> 27.3 us
  matrix products: 104 us -> 0.27 us
  local copies, waits for them, and re-layouts: 93.6 us -> 42.6 us
  Pallas kernels: 0 us -> 48.9 us
  blocking collectives: 76.4 us -> 39.6 us
  starting transfers between devices: 10.3 us -> 37.9 us
    all_gather x2 -> x0, waiting for transfers between devices: 1240 us -> none  [carried_in(): pieces = jax.tree.map(lambda part: lax.all_gather(part, axis), value)]
    select_n x31 -> x2, other arithmetic: 179 us -> 2.59 us  [chain(): carried = jnp.where(mine == step, arrived, carried)]
    dot_general x8 -> x1, matrix products: 104 us -> 0.27 us  [body(): sums = jnp.einsum('bhkj,ij->bhki', both, upto, precision=HIGH)]
    all_to_all x0 -> x4, waiting for transfers between devices: none -> 66.7 us  [exchange(): return lax.all_to_all(array, inner, 0, 0, tiled=True)]
    ppermute x3 -> x9, waiting for transfers between devices: 3.87 us -> 68.7 us  [the longest x6 61.5 us: chain(): arrived = lax.ppermute(leaving, axis, [(source, goal)])]
    pallas_call x0 -> x2, Pallas kernels: none -> 48.9 us  [the longest x1 35 us: main(): pl.pallas_call(functools.partial(main_kernel, heads, count), grid=(pairs,...]
    rev x2 -> x0, local copies, waits for them, and re-layouts: 44.2 us -> none  [carried_in(): pieces = jax.tree.map(lambda part: part[::-1], pieces)]
    all_gather x1 -> x0, blocking collectives: 38.1 us -> none  [carried_in(): pieces = jax.tree.map(lambda part: lax.all_gather(part, axis), value)]
  transfers between devices with their start and end apart: 5 -> 13, of which waited for: 3 -> 6; matrix products, arithmetic and copies ran while one was open for 2% -> 10% of each run, Pallas kernels for 0% -> 0%
where the time goes in v1:
time: 338 us; the launch traced here: 336 us
  waiting for transfers between devices  135 us (40%)
  Pallas kernels  48.9 us (14%)
  local copies, waits for them, and re-layouts  42.6 us (13%)
  blocking collectives  39.6 us (12%)
  starting transfers between devices  37.9 us (11%)
  other arithmetic  27.3 us (8%)
  between operations  4.28 us (1%)
    all_to_all x4, waiting for transfers between devices, exchange(): return lax.all_to_all(array, inner, 0, 0, tiled=True)  66.7 us
    ppermute x6, waiting for transfers between devices, chain(): arrived = lax.ppermute(leaving, axis, [(source, goal)])  61.5 us
    psum x1, blocking collectives, body(): totals = lax.psum(jnp.sum(score, axis=(1, 2)), (outer, inner, 'head'))  39.6 us
    pallas_call x1, Pallas kernels, main(): pl.pallas_call(functools.partial(main_kernel, heads, count), grid=(pairs,...  35 us
    all_to_all x4, starting transfers between devices, exchange(): return lax.all_to_all(array, inner, 0, 0, tiled=True)  18 us
    unnamed x21, local copies, waits for them, and re-layouts  15.1 us
    pallas_call x1, Pallas kernels, ends(): pl.pallas_call(functools.partial(ends_kernel, heads, rows // SPAN), grid=...  13.9 us
    ppermute x6, starting transfers between devices, chain(): arrived = lax.ppermute(leaving, axis, [(source, goal)])  11.6 us
  transfers between devices with their start and end apart: 13, of which 6 were waited for; matrix products, arithmetic and copies ran while one was open for 10% of the time, Pallas kernels for 0%

profile of v1, /device:TPU:0, one launch (start us, length us, event | category | flops | bytes accessed | tf_op | source)
XLA Modules:
  0.0 336.3 jit_solution(17363169954567176975)
XLA Ops:
  1.4 0.9 copy.92
  2.9 5.2 %all-to-all-start.1 = ((f32[4,2,17,128]{3,1,2,0:T(2,128)}), f32[4,2,17,128]{3,1,2,0:T(2,128)S(1)}, u32[]{:S(2)}, u32[]{:S(2)}) async-start(f32[4,2,17,128]{3,1,2,0:T(2,128)} %maximum_bitcast_fusion.1), calls=%async_computation.1 | async-start | bytes 139264 | tf_op jit(solution)/shard_map/all_to_all | solution.py:303
  8.1 1.1 copy.89
  9.2 1.1 copy.88
  10.4 3.1 copy.87
  13.5 4.1 %copy.86 = bf16[2,128,4096]{1,2,0:T(8,128)(2,1)} copy(bf16[2,128,4096]{2,1,0:T(8,128)(2,1)} %param.9) | data formatting | bytes 4194304 | tf_op args[0]
  17.6 1.7 maximum_bitcast_fusion
  19.3 2.4 copy.90
  21.8 5.1 %all-to-all-start = ((bf16[4,2,128,2304]{2,3,1,0:T(8,128)(2,1)}), bf16[4,2,128,2304]{2,3,1,0:T(8,128)(2,1)}, u32[]{:S(2)}, u32[]{:S(2)}) async-start(bf16[4,2,128,2304]{2,3,1,0:T(8,128)(2,1)} %copy.90), calls=%async_computation | async-start | bytes 9437184 | tf_op jit(solution)/shard_map/all_to_all | solution.py:303
  29.0 3.5 %collective-permute-start.1 = (f32[2,2]{1,0:T(2,128)S(1)}, f32[2,2]{1,0:T(2,128)S(1)}, u32[]{:S(2)}, u32[]{:S(2)}) collective-permute-start(f32[2,2]{1,0:T(2,128)S(1)} %slice.96), channel_id=1, source_target_pairs={{0,8},{8,16},{16,24},{1,9},{9,17},{17,25},{2,10},{10,18},{18,26},{... | collective-permute-start | bytes 56 | tf_op jit(solution)/shard_map/ppermute | solution.py:326
  34.3 1.0 copy.110.tok_ref
  35.3 44.6 %all-to-all-done = bf16[4,2,128,2304]{2,3,1,0:T(8,128)(2,1)} async-done(((bf16[4,2,128,2304]{2,3,1,0:T(8,128)(2,1)}), bf16[4,2,128,2304]{2,3,1,0:T(8,128)(2,1)}, u32[]{:S(2)}, u32[]{:S(2)}) %all-to-all-start) | async-done | bytes 4718624 | tf_op jit(solution)/shard_map/all_to_all | solution.py:303
  79.9 2.8 copy_bitcast_fusion
  82.7 1.6 fusion.15
  84.5 3.5 %collective-permute-start = (bf16[2,16,1024]{1,2,0:T(8,128)(2,1)S(1)}, bf16[2,16,1024]{1,2,0:T(8,128)(2,1)S(1)}, u32[]{:S(2)}, u32[]{:S(2)}) collective-permute-start(bf16[2,16,1024]{1,2,0:T(8,128)(2,1)S(1)} %slice.85), channel_id=1, source_target_pairs={{0,8},{8,16},{16,24},{1,9},{9,17},{17,25},{2,10},{10,18},{18,26},{... | collective-permute-start | bytes 196616 | tf_op jit(solution)/shard_map/ppermute | solution.py:325
  88.1 1.0 slice_bitcast_fusion.4
  89.0 2.5 copy.107.t_ref
  91.5 6.9 %collective-permute-done = bf16[2,16,1024]{1,2,0:T(8,128)(2,1)S(1)} collective-permute-done((bf16[2,16,1024]{1,2,0:T(8,128)(2,1)S(1)}, bf16[2,16,1024]{1,2,0:T(8,128)(2,1)S(1)}, u32[]{:S(2)}, u32[]{:S(2)}) %collective-permute-start) | collective-permute-done | bytes 65568 | tf_op jit(solution)/shard_map/ppermute | solution.py:325
  98.4 3.0 pad_maximum_fusion.1
  101.4 2.6 copy.106.x_ref
  104.0 13.9 %ends.1 = (f32[2,128,1024]{2,1,0:T(8,128)}, f32[2,128,1024]{2,1,0:T(8,128)}) custom-call(bf16[2,528,1024]{2,1,0:T(8,128)(2,1)} %copy.106.x_ref, bf16[2,512,1024]{2,1,0:T(8,128)(2,1)} %copy.107.t_ref, bf16[2,128,512]{2,1,0:T(8,128)(2,1)} %get-tuple-element.22.bt_ref, bf16[2,128,512]{2,1,0:T(8,128)(2,1)} %get-tuple-element.21.ct_ref, ...), custom_call_target="tpu_custom_call" | custom-call | tf_op jit(solution)/shard_map/ends/pallas_call | solution.py:222
  117.9 3.3 broadcast_add_fusion
  121.9 4.5 %collective-permute-start.2 = (f32[2,128,1024]{2,1,0:T(8,128)}, f32[2,128,1024]{2,1,0:T(8,128)S(1)}, u32[]{:S(2)}, u32[]{:S(2)}) collective-permute-start(f32[2,128,1024]{2,1,0:T(8,128)} %get-tuple-element.41), channel_id=1, source_target_pairs={{0,8},{1,9},{2,10},{3,11},{4,12},{5,13},{6,14},{7,15}} | collective-permute-start | bytes 3145736 | tf_op jit(solution)/shard_map/ppermute | solution.py:282
  126.4 21.0 %collective-permute-done.2 = f32[2,128,1024]{2,1,0:T(8,128)S(1)} collective-permute-done((f32[2,128,1024]{2,1,0:T(8,128)}, f32[2,128,1024]{2,1,0:T(8,128)S(1)}, u32[]{:S(2)}, u32[]{:S(2)}) %collective-permute-start.2) | collective-permute-done | bytes 1048608 | tf_op jit(solution)/shard_map/ppermute | solution.py:282
  147.4 3.0 multiply_add_fusion.1
  150.4 1.6 collective-permute-start.6
  152.1 1.6 collective-permute-start.3
  153.7 3.3 multiply_add_fusion
  157.0 1.6 collective-permute-start.4
  158.6 1.5 collective-permute-start.7
  161.3 1.8 copy.108.b_ref
  163.9 1.3 broadcast_select_fusion.1.start_ref
  165.2 40.5 %collective-permute-done.7 = f32[2,128,1024]{2,1,0:T(8,128)S(1)} collective-permute-done((f32[2,128,1024]{2,1,0:T(8,128)}, f32[2,128,1024]{2,1,0:T(8,128)S(1)}, u32[]{:S(2)}, u32[]{:S(2)}) %collective-permute-start.7) | collective-permute-done | bytes 1048608 | tf_op jit(solution)/shard_map/ppermute | solution.py:282
  205.8 1.3 broadcast_select_fusion.later_ref
  207.0 35.0 %main.1 = (f32[2,528,1024]{2,1,0:T(8,128)}, f32[2,512,128]{2,1,0:T(8,128)}, f32[2,8,1024]{2,1,0:T(8,128)}) custom-call(bf16[2,528,1024]{2,1,0:T(8,128)(2,1)} %copy.106.x_ref, bf16[2,512,1024]{2,1,0:T(8,128)(2,1)} %copy.107.t_ref, bf16[2,512,128]{2,1,0:T(8,128)(2,1)} %copy.108.b_ref, bf16[2,512,128]{2,1,0:T(8,128)(2,1)} %copy.109.c_ref, ...), custom_call_target="tpu_custom_call" | custom-call | tf_op jit(solution)/shard_map/main/pallas_call | solution.py:241
  242.1 0.9 reduce_sum.18
  243.0 1.0 slice.83
  244.0 4.7 %slice.81 = f32[2,496,1024]{2,1,0:T(8,128)} slice(f32[2,528,1024]{2,1,0:T(8,128)} %get-tuple-element.11), slice={[0:2], [16:512], [0:1024]} | slice | bytes 8126464 | tf_op jit(solution)/shard_map/slice | solution.py:382
  248.7 39.6 %psum.7 = f32[2]{0:T(128)S(1)} all-reduce(f32[2]{0:T(128)S(1)} %reduce_sum.18), channel_id=1, replica_groups=mesh['outer'=4,'inner'=4,'head'=2] {'outer','inner','head'}, use_global_device_ids=true, to_apply=%region_2.3 | all-reduce | flops 2 | bytes 16 | tf_op jit(solution)/shard_map/psum | solution.py:373
  288.3 1.3 collective-permute-start.8
  291.9 3.5 %all-to-all-start.3 = ((f32[4,2,16,128]{3,1,2,0:T(2,128)}), f32[4,2,16,128]{3,1,2,0:T(2,128)S(1)}, u32[]{:S(2)}, u32[]{:S(2)}) async-start(f32[4,2,16,128]{3,1,2,0:T(2,128)} %bitcast_bitcast_fusion), calls=%async_computation.3 | async-start | bytes 131072 | tf_op jit(solution)/shard_map/all_to_all | solution.py:303
  295.5 0.9 slice_add_fusion
  296.4 2.5 pad_maximum_fusion
  298.9 2.0 fusion.1
  300.8 4.2 %all-to-all-start.2 = ((bf16[4,2,128,1024]{3,2,1,0:T(8,128)(2,1)}), bf16[4,2,128,1024]{3,2,1,0:T(8,128)(2,1)S(1)}, u32[]{:S(2)}, u32[]{:S(2)}) async-start(bf16[4,2,128,1024]{3,2,1,0:T(8,128)(2,1)} %fusion.1), calls=%async_computation.2 | async-start | bytes 4194304 | tf_op jit(solution)/shard_map/all_to_all | solution.py:303
  306.4 22.1 %all-to-all-done.2 = bf16[4,2,128,1024]{3,2,1,0:T(8,128)(2,1)S(1)} async-done(((bf16[4,2,128,1024]{3,2,1,0:T(8,128)(2,1)}), bf16[4,2,128,1024]{3,2,1,0:T(8,128)(2,1)S(1)}, u32[]{:S(2)}, u32[]{:S(2)}) %all-to-all-start.2) | async-done | bytes 2097184 | tf_op jit(solution)/shard_map/all_to_all | solution.py:303
  328.5 2.6 copy.112
  331.1 4.1 %copy.115 = bf16[2,128,4096]{2,1,0:T(8,128)(2,1)} copy(bf16[2,128,4096]{1,2,0:T(8,128)(2,1)} %bitcast.83) | data formatting | bytes 4194304
  (66 shorter events, 9.7 us)
Async XLA Ops:
  0.6 26.3 %copy-start = (f32[4,4096]{1,0:T(4,128)S(1)}, f32[4,4096]{1,0:T(4,128)}, u32[]{:S(2)}) copy-start(f32[4,4096]{1,0:T(4,128)} %param.16) | copy-start | bytes 196612
  2.9 18.8 %all-to-all-start.1 = ((f32[4,2,17,128]{3,1,2,0:T(2,128)}), f32[4,2,17,128]{3,1,2,0:T(2,128)S(1)}, u32[]{:S(2)}, u32[]{:S(2)}) async-start(f32[4,2,17,128]{3,1,2,0:T(2,128)} %maximum_bitcast_fusion.1), calls=%async_computation.1 | async-start | bytes 139264 | tf_op jit(solution)/shard_map/all_to_all | solution.py:303
  21.8 5.1 %copy-start.6 = (f32[64]{0:T(128)S(1)}, f32[64]{0:T(128)}, u32[]{:S(2)}) copy-start(f32[64]{0:T(128)} %param.15) | copy-start | bytes 772
  21.8 58.1 %all-to-all-start = ((bf16[4,2,128,2304]{2,3,1,0:T(8,128)(2,1)}), bf16[4,2,128,2304]{2,3,1,0:T(8,128)(2,1)}, u32[]{:S(2)}, u32[]{:S(2)}) async-start(bf16[4,2,128,2304]{2,3,1,0:T(8,128)(2,1)} %copy.90), calls=%async_computation | async-start | bytes 9437184 | tf_op jit(solution)/shard_map/all_to_all | solution.py:303
  29.0 4.8 %collective-permute-start.1 = (f32[2,2]{1,0:T(2,128)S(1)}, f32[2,2]{1,0:T(2,128)S(1)}, u32[]{:S(2)}, u32[]{:S(2)}) collective-permute-start(f32[2,2]{1,0:T(2,128)S(1)} %slice.96), channel_id=1, source_target_pairs={{0,8},{8,16},{16,24},{1,9},{9,17},{17,25},{2,10},{10,18},{18,26},{... | collective-permute-start | bytes 56 | tf_op jit(solution)/shard_map/ppermute | solution.py:326
  34.3 45.6 %copy-start.3 = (f32[2,128,512]{2,1,0:T(8,128)}, f32[2,128,512]{2,1,0:T(8,128)S(1)}, u32[]{:S(2)}) copy-start(f32[2,128,512]{2,1,0:T(8,128)S(1)} %concatenate.28.row_ref) | copy-start | bytes 1572868
  84.5 13.9 %collective-permute-start = (bf16[2,16,1024]{1,2,0:T(8,128)(2,1)S(1)}, bf16[2,16,1024]{1,2,0:T(8,128)(2,1)S(1)}, u32[]{:S(2)}, u32[]{:S(2)}) collective-permute-start(bf16[2,16,1024]{1,2,0:T(8,128)(2,1)S(1)} %slice.85), channel_id=1, source_target_pairs={{0,8},{8,16},{16,24},{1,9},{9,17},{17,25},{2,10},{10,18},{18,26},{... | collective-permute-start | bytes 196616 | tf_op jit(solution)/shard_map/ppermute | solution.py:325
  101.4 16.5 %copy-start.5 = (f32[2,1024]{1,0:T(2,128)S(1)}, f32[2,1024]{1,0:T(2,128)}, u32[]{:S(2)}) copy-start(f32[2,1024]{1,0:T(2,128)} %broadcast_multiply_fusion) | copy-start | bytes 24580
  117.9 29.5 %copy-start.2 = (f32[2,128,1024]{2,1,0:T(8,128)S(1)}, f32[2,128,1024]{2,1,0:T(8,128)}, u32[]{:S(2)}) copy-start(f32[2,128,1024]{2,1,0:T(8,128)} %get-tuple-element.8) | copy-start | bytes 3145732
  121.2 5.2 %collective-permute-start.5 = (f32[2,128,1024]{2,1,0:T(8,128)}, f32[2,128,1024]{2,1,0:T(8,128)S(1)}, u32[]{:S(2)}, u32[]{:S(2)}) collective-permute-start(f32[2,128,1024]{2,1,0:T(8,128)} %get-tuple-element.40), channel_id=1, source_target_pairs={{24,16},{25,17},{26,18},{27,19},{28,20},{29,21},{30,22},{31,23}} | collective-permute-start | bytes 3145736 | tf_op jit(solution)/shard_map/ppermute | solution.py:282
  121.9 25.5 %collective-permute-start.2 = (f32[2,128,1024]{2,1,0:T(8,128)}, f32[2,128,1024]{2,1,0:T(8,128)S(1)}, u32[]{:S(2)}, u32[]{:S(2)}) collective-permute-start(f32[2,128,1024]{2,1,0:T(8,128)} %get-tuple-element.41), channel_id=1, source_target_pairs={{0,8},{1,9},{2,10},{3,11},{4,12},{5,13},{6,14},{7,15}} | collective-permute-start | bytes 3145736 | tf_op jit(solution)/shard_map/ppermute | solution.py:282
  150.4 3.3 collective-permute-start.6
  152.1 1.6 collective-permute-start.3
  157.0 6.9 %collective-permute-start.4 = (f32[2,128,1024]{2,1,0:T(8,128)}, f32[2,128,1024]{2,1,0:T(8,128)}, u32[]{:S(2)}, u32[]{:S(2)}) collective-permute-start(f32[2,128,1024]{2,1,0:T(8,128)} %get-tuple-element.37), channel_id=1, source_target_pairs={{16,24},{17,25},{18,26},{19,27},{20,28},{21,29},{22,30},{23,31}} | collective-permute-start | bytes 3145736 | tf_op jit(solution)/shard_map/ppermute | solution.py:282
  158.6 47.1 %collective-permute-start.7 = (f32[2,128,1024]{2,1,0:T(8,128)}, f32[2,128,1024]{2,1,0:T(8,128)S(1)}, u32[]{:S(2)}, u32[]{:S(2)}) collective-permute-start(f32[2,128,1024]{2,1,0:T(8,128)} %get-tuple-element.36), channel_id=1, source_target_pairs={{8,0},{9,1},{10,2},{11,3},{12,4},{13,5},{14,6},{15,7}} | collective-permute-start | bytes 3145736 | tf_op jit(solution)/shard_map/ppermute | solution.py:282
  243.0 47.9 %copy-start.4 = (f32[2,512,128]{2,1,0:T(8,128)S(1)}, f32[2,512,128]{2,1,0:T(8,128)}, u32[]{:S(2)}) copy-start(f32[2,512,128]{2,1,0:T(8,128)} %get-tuple-element.12) | copy-start | bytes 1572868
  288.3 7.2 %collective-permute-start.8 = (f32[2,16,1024]{2,1,0:T(8,128)S(1)}, f32[2,16,1024]{2,1,0:T(8,128)S(1)}, u32[]{:S(2)}, u32[]{:S(2)}) collective-permute-start(f32[2,16,1024]{2,1,0:T(8,128)S(1)} %slice.83), channel_id=1, source_target_pairs={{8,0},{16,8},{24,16},{9,1},{17,9},{25,17},{10,2},{18,10},{26,18},{... | collective-permute-start | bytes 393224 | tf_op jit(solution)/shard_map/ppermute | solution.py:380
  291.9 8.9 %all-to-all-start.3 = ((f32[4,2,16,128]{3,1,2,0:T(2,128)}), f32[4,2,16,128]{3,1,2,0:T(2,128)S(1)}, u32[]{:S(2)}, u32[]{:S(2)}) async-start(f32[4,2,16,128]{3,1,2,0:T(2,128)} %bitcast_bitcast_fusion), calls=%async_computation.3 | async-start | bytes 131072 | tf_op jit(solution)/shard_map/all_to_all | solution.py:303
  300.8 27.7 %all-to-all-start.2 = ((bf16[4,2,128,1024]{3,2,1,0:T(8,128)(2,1)}), bf16[4,2,128,1024]{3,2,1,0:T(8,128)(2,1)S(1)}, u32[]{:S(2)}, u32[]{:S(2)}) async-start(bf16[4,2,128,1024]{3,2,1,0:T(8,128)(2,1)} %fusion.1), calls=%async_computation.2 | async-start | bytes 4194304 | tf_op jit(solution)/shard_map/all_to_all | solution.py:303
  305.8 29.4 %copy-start.1 = (f32[4,4096]{1,0:T(4,128)S(1)}, f32[4,4096]{1,0:T(4,128)}, u32[]{:S(2)}) copy-start(f32[4,4096]{1,0:T(4,128)} %param.16) | copy-start | bytes 196612

commit v2 on v1

--- a/solution.py
+++ b/solution.py
@@ -13,6 +13,7 @@
 SPAN = 128
 LANES = 128
 TAPS = 4
+CUTS = 4
 HALO = 16
 FAR = -1e30
 HIGH = lax.Precision.HIGHEST
@@ -259,30 +260,232 @@
     )(x_ext, target, b_rows, c_rows, b_t, c_t, tok, table, taps, rate, start, later)
 
 
-def chain(through, alone, axis, backward):
+def send(source, goal, sent, got, where):
+    return pltpu.make_async_remote_copy(
+        src_ref=source,
+        dst_ref=goal,
+        send_sem=sent,
+        recv_sem=got,
+        device_id=where,
+        device_id_type=pl.DeviceIdType.MESH,
+    )
+
+
+def greet(barrier, where):
+    pl.semaphore_signal(barrier, inc=1, device_id=where, device_id_type=pl.DeviceIdType.MESH)
+
+
+def chain_kernel(axis, through_ref, alone_ref, seed_ref, start_ref, later_ref, out_scr, in_scr, sent, got):
     count = lax.axis_size(axis)
     mine = lax.axis_index(axis)
-    if backward:
-        mine = count - 1 - mine
-    carried = jnp.zeros_like(alone)
-
-    def hop(step, carried):
-        leaving = through * carried + alone
-        if backward:
-            route = [(i, i - 1) for i in range(1, count)]
-        else:
-            route = [(i, i + 1) for i in range(count - 1)]
-        arrived = lax.ppermute(leaving, axis, route)
-        return jnp.where(mine == step, arrived, carried)
-
-    if count <= 8:
-        for step in range(1, count):
-            leaving = through * carried + alone
-            source, goal = (count - step, count - step - 1) if backward else (step - 1, step)
-            arrived = lax.ppermute(leaving, axis, [(source, goal)])
-            carried = jnp.where(mine == step, arrived, carried)
-        return carried
-    return lax.fori_loop(1, count, hop, carried)
+    pairs, states, chans = alone_ref.shape
+    has_less = mine > 0
+    has_more = mine < count - 1
+    less = lax.rem(mine + count - 1, count)
+    more = lax.rem(mine + 1, count)
+    barrier = pltpu.get_barrier_semaphore()
+
+    @pl.when(has_less)
+    def _():
+        greet(barrier, {axis: less})
+
+    @pl.when(has_more)
+    def _():
+        greet(barrier, {axis: more})
+
+    pl.semaphore_wait(barrier, has_less.astype(jnp.int32) + has_more.astype(jnp.int32))
+    ways = ((alone_ref, has_less, has_more, more), (seed_ref, has_more, has_less, less))
+    for way, (_, arrives, _, _) in enumerate(ways):
+
+        @pl.when(jnp.logical_not(arrives))
+        def _():
+            in_scr[way] = jnp.zeros((pairs, states, chans), F32)
+
+    size = states // CUTS
+    copies = []
+    for b in range(pairs):
+        for cut in range(CUTS):
+            rows = pl.ds(cut * size, size)
+            piece = b * CUTS + cut
+            for way, (own, arrives, leaves, goal) in enumerate(ways):
+                copy = send(
+                    out_scr.at[way, b, rows], in_scr.at[way, b, rows], sent.at[way, piece], got.at[way, piece], {axis: goal}
+                )
+
+                @pl.when(arrives)
+                def _():
+                    copy.wait_recv()
+
+                @pl.when(leaves)
+                def _():
+                    out_scr[way, b, rows, :] = through_ref[b] * in_scr[way, b, rows, :] + own[b, rows, :]
+                    copy.start()
+
+                copies.append((copy, leaves))
+    start_ref[...] = in_scr[0]
+    later_ref[...] = in_scr[1]
+    for copy, leaves in copies:
+
+        @pl.when(leaves)
+        def _():
+            copy.wait_send()
+
+
+def chain(through, alone, seed, axis):
+    shape = jax.ShapeDtypeStruct(alone.shape, F32)
+    vmem = pl.BlockSpec(memory_space=pltpu.VMEM)
+    return pl.pallas_call(
+        functools.partial(chain_kernel, axis),
+        out_shape=(shape, shape),
+        in_specs=[vmem] * 3,
+        out_specs=(vmem, vmem),
+        scratch_shapes=[
+            pltpu.VMEM((2,) + alone.shape, F32),
+            pltpu.VMEM((2,) + alone.shape, F32),
+            pltpu.SemaphoreType.DMA((2, 2 * CUTS)),
+            pltpu.SemaphoreType.DMA((2, 2 * CUTS)),
+        ],
+        compiler_params=pltpu.CompilerParams(collective_id=0, has_side_effects=True),
+        name="chain",
+    )(through, alone, seed)
+
+
+def finish_kernel(
+    axes, size, grad_ref, score_ref, raw_ref, sign_ref, loss_ref, out_ref, slope_ref,
+    part_scr, slot_scr, halo_scr, out_scr, raw_scr, psent, pgot, hsent, hgot, osent, ogot, rsent, rgot,
+):
+    outer, inner, _ = axes
+    pairs, chans = grad_ref.shape[0], grad_ref.shape[2]
+    heads = raw_ref.shape[1]
+    rows = out_ref.shape[1]
+    parts, planes = lax.axis_size(inner), lax.axis_size(outer)
+    mine, plane = lax.axis_index(inner), lax.axis_index(outer)
+    row = lax.broadcasted_iota(jnp.int32, (8, LANES), 0)
+    own = [jnp.sum(jnp.sum(score_ref[b], axis=0, keepdims=True), axis=1, keepdims=True) for b in range(pairs)]
+    part_scr[0] = jnp.where(row == 0, own[0], own[1])
+    barrier = pltpu.get_barrier_semaphore()
+    peers = 0
+    for axis in axes:
+        for away in range(1, lax.axis_size(axis)):
+            greet(barrier, {axis: lax.rem(lax.axis_index(axis) + away, lax.axis_size(axis))})
+            peers += 1
+    pl.semaphore_wait(barrier, peers)
+    has_less = plane > 0
+    has_more = plane < planes - 1
+    edge = send(
+        grad_ref.at[:, pl.ds(0, HALO)], halo_scr, hsent, hgot, {outer: lax.rem(plane + planes - 1, planes)}
+    )
+
+    @pl.when(has_less)
+    def _():
+        edge.start()
+
+    waits = []
+    first = 0
+    for turn, axis in enumerate(axes[::-1]):
+        count = lax.axis_size(axis)
+        me = lax.axis_index(axis)
+        copies = []
+        for away in range(1, count):
+            goal = lax.rem(me + away, count)
+            spot = first + away - 1
+            copy = send(part_scr.at[turn], slot_scr.at[first + me], psent.at[spot], pgot.at[spot], {axis: goal})
+            copy.start()
+            copies.append(copy)
+        slot_scr[first + me] = part_scr[turn]
+        for copy in copies:
+            copy.wait_recv()
+        waits += copies
+        subtotal = slot_scr[first]
+        for i in range(1, count):
+            subtotal = subtotal + slot_scr[first + i]
+        part_scr[turn + 1] = subtotal
+        first += count
+    signed = subtotal * sign_ref[...] / math.sqrt(size)
+    margin = signed[0:1, :] + signed[1:2, :]
+    loss_ref[...] = jnp.broadcast_to(jax.nn.softplus(-margin), loss_ref.shape)
+    factors = -jax.nn.sigmoid(-margin) * sign_ref[...]
+    scale = [factors[b : b + 1, 0:1] for b in range(pairs)]
+
+    @pl.when(has_more)
+    def _():
+        edge.wait_recv()
+
+    @pl.when(jnp.logical_not(has_more))
+    def _():
+        halo_scr[...] = jnp.zeros_like(halo_scr)
+
+    columns = pl.ds(pl.multiple_of(mine * chans, LANES), chans)
+    lines = pl.ds(pl.multiple_of(mine * heads, 8), heads)
+    for away in range(parts):
+        goal = lax.rem(mine + away, parts) if parts > 1 else 0
+        begin = pl.multiple_of(goal * rows, SPAN)
+        last = jnp.where(goal == parts - 1, 1.0, 0.0).astype(F32)
+        for b in range(pairs):
+            body_rows = grad_ref[b, pl.ds(HALO + begin, rows - HALO), :]
+            edge_rows = grad_ref[b, pl.ds(begin + rows, HALO), :] + last * halo_scr[b]
+            above = (scale[b] * body_rows).astype(BF16)
+            below = (scale[b] * edge_rows).astype(BF16)
+            lean = scale[b] * raw_ref[b, :, pl.ds(begin, rows)]
+            if away == 0:
+                out_ref[b, pl.ds(0, rows - HALO), columns] = above
+                out_ref[b, pl.ds(rows - HALO, HALO), columns] = below
+                slope_ref[b, lines, :] = lean
+                continue
+            out_scr[away, b, pl.ds(0, rows - HALO), :] = above
+            out_scr[away, b, pl.ds(rows - HALO, HALO), :] = below
+            raw_scr[away, b] = lean
+        if away > 0:
+            wide = send(
+                out_scr.at[away], out_ref.at[:, :, columns], osent.at[away], ogot.at[away], {inner: goal}
+            )
+            thin = send(raw_scr.at[away], slope_ref.at[:, lines], rsent.at[away], rgot.at[away], {inner: goal})
+            thin.start()
+            wide.start()
+            waits += [thin, wide]
+    for copy in waits[-2 * (parts - 1) :] if parts > 1 else []:
+        copy.wait_recv()
+    for copy in waits:
+        copy.wait_send()
+
+    @pl.when(has_less)
+    def _():
+        edge.wait_send()
+
+
+def finish(grad, score, raw, sign, axes, size, rows):
+    pairs, chans, heads = grad.shape[0], grad.shape[2], raw.shape[1]
+    parts = lax.axis_size(axes[1])
+    slots = sum(lax.axis_size(axis) for axis in axes)
+    vmem = pl.BlockSpec(memory_space=pltpu.VMEM)
+    dma = pltpu.SemaphoreType.DMA
+    return pl.pallas_call(
+        functools.partial(finish_kernel, axes, size),
+        out_shape=(
+            jax.ShapeDtypeStruct((8, LANES), F32),
+            jax.ShapeDtypeStruct((pairs, rows, parts * chans), BF16),
+            jax.ShapeDtypeStruct((pairs, parts * heads, rows), F32),
+        ),
+        in_specs=[vmem] * 4,
+        out_specs=(vmem,) * 3,
+        scratch_shapes=[
+            pltpu.VMEM((len(axes) + 1, 8, LANES), F32),
+            pltpu.VMEM((slots, 8, LANES), F32),
+            pltpu.VMEM((pairs, HALO, chans), F32),
+            pltpu.VMEM((parts, pairs, rows, chans), BF16),
+            pltpu.VMEM((parts, pairs, heads, rows), F32),
+            dma((slots,)),
+            dma((slots,)),
+            dma,
+            dma,
+            dma((parts,)),
+            dma((parts,)),
+            dma((parts,)),
+            dma((parts,)),
+        ],
+        compiler_params=pltpu.CompilerParams(collective_id=1, has_side_effects=True),
+        name="finish",
+    )(grad, score, raw, sign)
 
 
 def body(outer, inner, x_in, target, b_in, c_in, dt_raw, resets, decay_rate, conv_w, label):
@@ -366,27 +569,15 @@
     c_t = c_all.transpose(0, 2, 1)
     alone, seed = ends(x_ext, t_all, b_t, c_t, tok, taps, heads)
     wide = jnp.repeat(through, width, axis=1)[:, None, :]
-    start = chain(wide, alone, outer, False)
-    later = chain(wide, seed, outer, True)
+    start, later = chain(wide, alone, seed, outer)
     rate_row = jnp.pad(rate, (0, LANES - heads))[None]
     grad, ddt, score = main(x_ext, t_all, b_all, c_all, b_t, c_t, tok, table, taps, rate_row, start, later, heads)
-    totals = lax.psum(jnp.sum(score, axis=(1, 2)), (outer, inner, "head"))
+    sign = jnp.where(jnp.arange(2) == label[0], 1.0, -1.0).astype(F32)
+    sign = jnp.broadcast_to(jnp.pad(sign, (0, 6))[:, None], (8, LANES))
     size = tokens * planes * x_in.shape[2] * lax.axis_size("head")
-    scores = totals / math.sqrt(size)
-    sign = jnp.where(jnp.arange(2) == label[0], 1.0, -1.0).astype(F32)
-    margin = jnp.sum(sign * scores)
-    loss = jax.nn.softplus(-margin)
-    factor = -jax.nn.sigmoid(-margin) * sign
-    back_rows = lax.ppermute(grad[:, :HALO], outer, [(i + 1, i) for i in range(planes - 1)])
-    grad = grad[:, HALO:]
-    grad = jnp.concatenate([grad[:, : tokens - HALO], grad[:, tokens - HALO :] + back_rows], axis=1)
-    grad = (factor[:, None, None] * grad).astype(BF16)
-    grad = exchange(grad.reshape(2, parts, rows, chans).transpose(1, 0, 2, 3))
-    grad = grad.transpose(1, 2, 0, 3).reshape(2, rows, parts * chans)
-    grad_raw = factor[:, None, None] * jax.nn.sigmoid(raw) * ddt[:, :, :heads].transpose(0, 2, 1)
-    grad_raw = exchange(grad_raw.reshape(2, heads, parts, rows).transpose(2, 0, 1, 3))
-    grad_raw = grad_raw.transpose(1, 0, 2, 3).reshape(2, all_heads, rows)
-    return (loss, grad, grad_raw)
+    lean = jax.nn.sigmoid(raw) * ddt[:, :, :heads].transpose(0, 2, 1)
+    loss, grad, grad_raw = finish(grad, score, lean, sign, (outer, inner, "head"), size, rows)
+    return (loss[0, 0], grad, grad_raw)
 
 
 def solution(mesh):

time: 338 us -> 398 us (1.18)
  Pallas kernels: 48.9 us -> 285 us
  waiting for transfers between devices: 135 us -> 49.6 us
  blocking collectives: 39.6 us -> 0 us
  starting transfers between devices: 37.9 us -> 17.3 us
  other arithmetic: 27.3 us -> 7.37 us
  local copies, waits for them, and re-layouts: 42.6 us -> 35.6 us
    pallas_call x0 -> x2, Pallas kernels: none -> 236 us  [the longest x1 199 us: chain(): pl.pallas_call(functools.partial(chain_kernel, axis), out_shape=(shape, s...]
    ppermute x7 -> x0, waiting for transfers between devices: 61.5 us -> none  [the longest x6 61.5 us: chain(): arrived = lax.ppermute(leaving, axis, [(source, goal)])]
    psum x1 -> x0, blocking collectives: 39.6 us -> none  [body(): totals = lax.psum(jnp.sum(score, axis=(1, 2)), (outer, inner, 'head'))]
    all_to_all x4 -> x2, waiting for transfers between devices: 66.7 us -> 44 us  [exchange(): return lax.all_to_all(array, inner, 0, 0, tiled=True)]
    ppermute x7 -> x0, starting transfers between devices: 12.8 us -> none  [the longest x6 11.6 us: chain(): arrived = lax.ppermute(leaving, axis, [(source, goal)])]
    add x4 -> x0, other arithmetic: 10.5 us -> none  [the longest x3 9.6 us: chain(): leaving = through * carried + alone]
    all_to_all x4 -> x2, starting transfers between devices: 18 us -> 10.3 us  [exchange(): return lax.all_to_all(array, inner, 0, 0, tiled=True)]
    slice x2, local copies, waits for them, and re-layouts: 5.63 us -> 1.19 us  [the longest x1 1.19 us: body(): return (loss[0, 0], grad, grad_raw)]
  transfers between devices with their start and end apart: 13 -> 4, of which waited for: 6 -> 2; matrix products, arithmetic and copies ran while one was open for 10% -> 5% of each run, Pallas kernels for 0% -> 0%
where the time goes in v2:
time: 398 us; the launch traced here: 397 us
  Pallas kernels  285 us (72%)
  waiting for transfers between devices  49.6 us (12%)
  local copies, waits for them, and re-layouts  35.6 us (9%)
  starting transfers between devices  17.3 us (4%)
  other arithmetic  7.37 us (2%)
    pallas_call x1, Pallas kernels, chain(): pl.pallas_call(functools.partial(chain_kernel, axis), out_shape=(shape, s...  199 us
    all_to_all x2, waiting for transfers between devices, exchange(): return lax.all_to_all(array, inner, 0, 0, tiled=True)  44 us
    pallas_call x1, Pallas kernels, finish(): pl.pallas_call(functools.partial(finish_kernel, axes, size), out_shape=(j...  37.1 us
    pallas_call x1, Pallas kernels, main(): pl.pallas_call(functools.partial(main_kernel, heads, count), grid=(pairs,...  35 us
    pallas_call x1, Pallas kernels, ends(): pl.pallas_call(functools.partial(ends_kernel, heads, rows // SPAN), grid=...  13.9 us
    unnamed x18, local copies, waits for them, and re-layouts  13.1 us
    all_to_all x2, starting transfers between devices, exchange(): return lax.all_to_all(array, inner, 0, 0, tiled=True)  10.3 us
  transfers between devices with their start and end apart: 4, of which 2 were waited for; matrix products, arithmetic and copies ran while one was open for 5% of the time, Pallas kernels for 0%

profile of v2, /device:TPU:0, one launch (start us, length us, event | category | flops | bytes accessed | tf_op | source)
XLA Modules:
  0.0 397.1 jit_solution(14696075030912337834)
XLA Ops:
  0.7 1.0 copy.85
  1.6 0.7 convert_element_type.5
  2.3 0.7 maximum_bitcast_fusion.1
  3.0 5.2 %all-to-all-start.1 = ((f32[4,2,17,128]{3,1,2,0:T(2,128)}), f32[4,2,17,128]{3,1,2,0:T(2,128)S(1)}, u32[]{:S(2)}, u32[]{:S(2)}) async-start(f32[4,2,17,128]{3,1,2,0:T(2,128)} %maximum_bitcast_fusion.1), calls=%async_computation.1 | async-start | bytes 139264 | tf_op jit(solution)/shard_map/all_to_all | solution.py:506
  8.2 3.1 copy.79
  11.3 4.1 %copy.80 = bf16[2,128,4096]{1,2,0:T(8,128)(2,1)} copy(bf16[2,128,4096]{2,1,0:T(8,128)(2,1)} %param.10) | data formatting | bytes 4194304 | tf_op args[1]
  15.4 0.2 copy.81
  15.6 0.2 copy.82
  15.7 1.7 maximum_bitcast_fusion
  17.5 2.5 copy.83
  19.9 5.1 %all-to-all-start = ((bf16[4,2,128,2304]{2,3,1,0:T(8,128)(2,1)}), bf16[4,2,128,2304]{2,3,1,0:T(8,128)(2,1)}, u32[]{:S(2)}, u32[]{:S(2)}) async-start(bf16[4,2,128,2304]{2,3,1,0:T(8,128)(2,1)} %copy.83), calls=%async_computation | async-start | bytes 9437184 | tf_op jit(solution)/shard_map/all_to_all | solution.py:506
  25.7 0.1 dynamic_slice.6
  25.8 0.5 pad_bitcast_fusion.rate_ref
  26.3 0.6 constant_dynamic-slice_fusion.w_ref
  27.0 0.1 negate_multiply_fusion
  27.2 3.5 collective-permute-start.1
  30.7 0.3 fusion
  31.0 0.2 slice_reduce_fusion.2
  31.1 0.2 slice_reduce_fusion.1
  31.3 0.1 compare_convert_fusion
  31.4 0.1 slice_bitcast_fusion.1
  31.5 0.2 slice_reduce_fusion
  31.8 0.7 broadcast_in_dim_reshape.3.through_ref
  32.6 0.1 fusion.7
  32.8 0.3 concatenate.23.row_ref
  33.0 1.0 copy.104.tok_ref
  34.1 44.0 %all-to-all-done = bf16[4,2,128,2304]{2,3,1,0:T(8,128)(2,1)} async-done(((bf16[4,2,128,2304]{2,3,1,0:T(8,128)(2,1)}), bf16[4,2,128,2304]{2,3,1,0:T(8,128)(2,1)}, u32[]{:S(2)}, u32[]{:S(2)}) %all-to-all-start) | async-done | bytes 4718624 | tf_op jit(solution)/shard_map/all_to_all | solution.py:506
  78.1 2.8 copy_bitcast_fusion
  80.9 1.6 fusion.13
  82.5 1.1 slice.74
  83.6 3.5 collective-permute-start
  87.1 0.9 slice_bitcast_fusion.3
  88.0 2.5 copy.101.t_ref
  90.5 0.8 copy.102.b_ref
  91.3 0.8 copy.103.c_ref
  92.1 5.6 %collective-permute-done = bf16[2,16,1024]{1,2,0:T(8,128)(2,1)S(1)} collective-permute-done((bf16[2,16,1024]{1,2,0:T(8,128)(2,1)}, bf16[2,16,1024]{1,2,0:T(8,128)(2,1)S(1)}, u32[]{:S(2)}, u32[]{:S(2)}) %collective-permute-start) | collective-permute-done | bytes 65568 | tf_op jit(solution)/shard_map/ppermute | solution.py:528
  97.8 3.0 pad_maximum_fusion
  100.8 2.6 copy.100.x_ref
  103.4 13.9 %ends.1 = (f32[2,128,1024]{2,1,0:T(8,128)}, f32[2,128,1024]{2,1,0:T(8,128)}) custom-call(bf16[2,528,1024]{2,1,0:T(8,128)(2,1)} %copy.100.x_ref, bf16[2,512,1024]{2,1,0:T(8,128)(2,1)} %copy.101.t_ref, bf16[2,128,512]{2,1,0:T(8,128)(2,1)} %get-tuple-element.24.bt_ref, bf16[2,128,512]{2,1,0:T(8,128)(2,1)} %get-tuple-element.23.ct_ref, ...), custom_call_target="tpu_custom_call" | custom-call | tf_op jit(solution)/shard_map/ends/pallas_call | solution.py:223
  117.3 199.3 %chain.1 = (f32[2,128,1024]{2,1,0:T(8,128)}, f32[2,128,1024]{2,1,0:T(8,128)}) custom-call(f32[2,1,1024]{2,1,0:T(1,128)} %broadcast_in_dim_reshape.3.through_ref, f32[2,128,1024]{2,1,0:T(8,128)} %get-tuple-element.13.alone_ref, f32[2,128,1024]{2,1,0:T(8,128)} %get-tuple-element.14.seed_ref), custom_call_target="tpu_custom_call" | custom-call | tf_op jit(solution)/shard_map/chain/pallas_call | solution.py:337
  316.6 35.0 %main.1 = (f32[2,528,1024]{2,1,0:T(8,128)}, f32[2,512,128]{2,1,0:T(8,128)}, f32[2,8,1024]{2,1,0:T(8,128)}) custom-call(bf16[2,528,1024]{2,1,0:T(8,128)(2,1)} %copy.100.x_ref, bf16[2,512,1024]{2,1,0:T(8,128)(2,1)} %copy.101.t_ref, bf16[2,512,128]{2,1,0:T(8,128)(2,1)} %copy.102.b_ref, bf16[2,512,128]{2,1,0:T(8,128)(2,1)} %copy.103.c_ref, ...), custom_call_target="tpu_custom_call" | custom-call | tf_op jit(solution)/shard_map/main/pallas_call | solution.py:242
  351.6 1.2 copy.105
  352.9 0.7 fusion.2.raw_ref
  353.5 0.7 broadcast_in_dim.57.sign_ref
  354.2 37.1 %finish.1 = (f32[8,128]{1,0:T(8,128)}, bf16[2,128,4096]{2,1,0:T(8,128)(2,1)}, f32[2,64,128]{2,1,0:T(8,128)}) custom-call(f32[2,528,1024]{2,1,0:T(8,128)} %get-tuple-element.17.grad_ref, f32[2,8,1024]{2,1,0:T(8,128)} %get-tuple-element.18.score_ref, f32[2,16,512]{2,1,0:T(8,128)} %fusion.2.raw_ref, f32[8,128]{1,0:T(8,128)} %broadcast_in_dim.57.sign_ref), custom_call_target="tpu_custom_call" | custom-call | tf_op jit(solution)/shard_map/finish/pallas_call | solution.py:462
  391.3 1.2 slice.73
  392.5 3.1 copy.129
  395.7 1.5 copy.130
  (32 shorter events, 0.5 us)
Async XLA Ops:
  0.6 25.7 %copy-start = (f32[4,4096]{1,0:T(4,128)S(1)}, f32[4,4096]{1,0:T(4,128)}, u32[]{:S(2)}) copy-start(f32[4,4096]{1,0:T(4,128)} %param.16) | copy-start | bytes 196612
  0.6 14.7 %copy-start.2 = (bf16[2,128,512]{2,1,0:T(8,128)(2,1)S(1)}, bf16[2,128,512]{2,1,0:T(8,128)(2,1)}, u32[]{:S(2)}) copy-start(bf16[2,128,512]{2,1,0:T(8,128)(2,1)} %param.11) | copy-start | bytes 786436
  0.7 14.9 %copy-start.3 = (bf16[2,128,512]{2,1,0:T(8,128)(2,1)S(1)}, bf16[2,128,512]{2,1,0:T(8,128)(2,1)}, u32[]{:S(2)}) copy-start(bf16[2,128,512]{2,1,0:T(8,128)(2,1)} %param.12) | copy-start | bytes 786436
  3.0 17.0 %all-to-all-start.1 = ((f32[4,2,17,128]{3,1,2,0:T(2,128)}), f32[4,2,17,128]{3,1,2,0:T(2,128)S(1)}, u32[]{:S(2)}, u32[]{:S(2)}) async-start(f32[4,2,17,128]{3,1,2,0:T(2,128)} %maximum_bitcast_fusion.1), calls=%async_computation.1 | async-start | bytes 139264 | tf_op jit(solution)/shard_map/all_to_all | solution.py:506
  19.9 5.8 %copy-start.4 = (f32[64]{0:T(128)S(1)}, f32[64]{0:T(128)}, u32[]{:S(2)}) copy-start(f32[64]{0:T(128)} %param.15) | copy-start | bytes 772
  19.9 58.1 %all-to-all-start = ((bf16[4,2,128,2304]{2,3,1,0:T(8,128)(2,1)}), bf16[4,2,128,2304]{2,3,1,0:T(8,128)(2,1)}, u32[]{:S(2)}, u32[]{:S(2)}) async-start(bf16[4,2,128,2304]{2,3,1,0:T(8,128)(2,1)} %copy.83), calls=%async_computation | async-start | bytes 9437184 | tf_op jit(solution)/shard_map/all_to_all | solution.py:506
  27.2 5.3 %collective-permute-start.1 = (f32[2,2]{1,0:T(2,128)S(1)}, f32[2,2]{1,0:T(2,128)S(1)}, u32[]{:S(2)}, u32[]{:S(2)}) collective-permute-start(f32[2,2]{1,0:T(2,128)S(1)} %slice.85), channel_id=1, source_target_pairs={{0,8},{8,16},{16,24},{1,9},{9,17},{17,25},{2,10},{10,18},{18,26},{... | collective-permute-start | bytes 56 | tf_op jit(solution)/shard_map/ppermute | solution.py:529
  33.0 47.9 %copy-start.1 = (f32[2,128,512]{2,1,0:T(8,128)}, f32[2,128,512]{2,1,0:T(8,128)S(1)}, u32[]{:S(2)}) copy-start(f32[2,128,512]{2,1,0:T(8,128)S(1)} %concatenate.23.row_ref) | copy-start | bytes 1572868
  83.6 14.2 %collective-permute-start = (bf16[2,16,1024]{1,2,0:T(8,128)(2,1)}, bf16[2,16,1024]{1,2,0:T(8,128)(2,1)S(1)}, u32[]{:S(2)}, u32[]{:S(2)}) collective-permute-start(bf16[2,16,1024]{1,2,0:T(8,128)(2,1)} %slice.74), channel_id=1, source_target_pairs={{0,8},{8,16},{16,24},{1,9},{9,17},{17,25},{2,10},{10,18},{18,26},{... | collective-permute-start | bytes 196616 | tf_op jit(solution)/shard_map/ppermute | solution.py:528

commit v3 on v2

--- a/solution.py
+++ b/solution.py
@@ -278,7 +278,7 @@
 def chain_kernel(axis, through_ref, alone_ref, seed_ref, start_ref, later_ref, out_scr, in_scr, sent, got):
     count = lax.axis_size(axis)
     mine = lax.axis_index(axis)
-    pairs, states, chans = alone_ref.shape
+    own_pieces, size, chans = alone_ref.shape
     has_less = mine > 0
     has_more = mine < count - 1
     less = lax.rem(mine + count - 1, count)
@@ -299,17 +299,18 @@
 
         @pl.when(jnp.logical_not(arrives))
         def _():
-            in_scr[way] = jnp.zeros((pairs, states, chans), F32)
-
-    size = states // CUTS
-    copies = []
-    for b in range(pairs):
-        for cut in range(CUTS):
-            rows = pl.ds(cut * size, size)
-            piece = b * CUTS + cut
-            for way, (own, arrives, leaves, goal) in enumerate(ways):
+            in_scr[way] = jnp.zeros((own_pieces, size, chans), F32)
+
+    pieces = own_pieces
+
+    def hop(time, carry):
+        for way, (own, arrives, leaves, goal) in enumerate(ways):
+            piece = time - (mine if way == 0 else count - 1 - mine)
+
+            @pl.when((piece >= 0) & (piece < pieces))
+            def _():
                 copy = send(
-                    out_scr.at[way, b, rows], in_scr.at[way, b, rows], sent.at[way, piece], got.at[way, piece], {axis: goal}
+                    out_scr.at[way, piece], in_scr.at[way, piece], sent.at[way, piece], got.at[way, piece], {axis: goal}
                 )
 
                 @pl.when(arrives)
@@ -318,23 +319,38 @@
 
                 @pl.when(leaves)
                 def _():
-                    out_scr[way, b, rows, :] = through_ref[b] * in_scr[way, b, rows, :] + own[b, rows, :]
+                    through = through_ref[piece // CUTS]
+                    out_scr[way, piece] = through * in_scr[way, piece] + own[piece]
                     copy.start()
 
-                copies.append((copy, leaves))
+        return carry
+
+    lax.fori_loop(0, pieces + count - 1, hop, 0)
     start_ref[...] = in_scr[0]
     later_ref[...] = in_scr[1]
-    for copy, leaves in copies:
-
-        @pl.when(leaves)
-        def _():
-            copy.wait_send()
+
+    def drain(piece, carry):
+        for way, (_, _, leaves, goal) in enumerate(ways):
+
+            @pl.when(leaves)
+            def _():
+                send(
+                    out_scr.at[way, piece], in_scr.at[way, piece], sent.at[way, piece], got.at[way, piece], {axis: goal}
+                ).wait_send()
+
+        return carry
+
+    lax.fori_loop(0, pieces, drain, 0)
 
 
 def chain(through, alone, seed, axis):
+    whole_shape = alone.shape
+    pieces = whole_shape[0] * CUTS
+    alone = alone.reshape(pieces, -1, whole_shape[2])
+    seed = seed.reshape(alone.shape)
     shape = jax.ShapeDtypeStruct(alone.shape, F32)
     vmem = pl.BlockSpec(memory_space=pltpu.VMEM)
-    return pl.pallas_call(
+    start, later = pl.pallas_call(
         functools.partial(chain_kernel, axis),
         out_shape=(shape, shape),
         in_specs=[vmem] * 3,
@@ -342,12 +358,13 @@
         scratch_shapes=[
             pltpu.VMEM((2,) + alone.shape, F32),
             pltpu.VMEM((2,) + alone.shape, F32),
-            pltpu.SemaphoreType.DMA((2, 2 * CUTS)),
-            pltpu.SemaphoreType.DMA((2, 2 * CUTS)),
+            pltpu.SemaphoreType.DMA((2, pieces)),
+            pltpu.SemaphoreType.DMA((2, pieces)),
         ],
         compiler_params=pltpu.CompilerParams(collective_id=0, has_side_effects=True),
         name="chain",
     )(through, alone, seed)
+    return start.reshape(whole_shape), later.reshape(whole_shape)
 
 
 def finish_kernel(

time: 398 us -> 245 us (0.62)
  Pallas kernels: 285 us -> 133 us
    pallas_call x1, Pallas kernels: 199 us -> 45.8 us  [chain(): pl.pallas_call(functools.partial(chain_kernel, axis), out_shape=(shape, s...]
  transfers between devices with their start and end apart: 4 -> 4, of which waited for: 2 -> 2; matrix products, arithmetic and copies ran while one was open for 5% -> 9% of each run, Pallas kernels for 0% -> 0%
where the time goes in v3:
time: 245 us; the launch traced here: 244 us
  Pallas kernels  133 us (54%)
  waiting for transfers between devices  49.6 us (20%)
  local copies, waits for them, and re-layouts  35.6 us (15%)
  starting transfers between devices  17.3 us (7%)
  other arithmetic  7.37 us (3%)
    pallas_call x1, Pallas kernels, chain(): pl.pallas_call(functools.partial(chain_kernel, axis), out_shape=(shape, s...  45.8 us
    all_to_all x2, waiting for transfers between devices, exchange(): return lax.all_to_all(array, inner, 0, 0, tiled=True)  44 us
    pallas_call x1, Pallas kernels, finish(): pl.pallas_call(functools.partial(finish_kernel, axes, size), out_shape=(j...  37.9 us
    pallas_call x1, Pallas kernels, main(): pl.pallas_call(functools.partial(main_kernel, heads, count), grid=(pairs,...  35 us
    pallas_call x1, Pallas kernels, ends(): pl.pallas_call(functools.partial(ends_kernel, heads, rows // SPAN), grid=...  13.9 us
    unnamed x18, local copies, waits for them, and re-layouts  13.1 us
    all_to_all x2, starting transfers between devices, exchange(): return lax.all_to_all(array, inner, 0, 0, tiled=True)  10.3 us
    ppermute x1, waiting for transfers between devices, body(): edge_rows = lax.ppermute(x_all[:, tokens - HALO:], outer, ahead)  5.63 us
  transfers between devices with their start and end apart: 4, of which 2 were waited for; matrix products, arithmetic and copies ran while one was open for 9% of the time, Pallas kernels for 0%

profile of v3, /device:TPU:0, one launch (start us, length us, event | category | flops | bytes accessed | tf_op | source)
XLA Modules:
  0.0 244.4 jit_solution(8262992396774557876)
XLA Ops:
  0.7 1.0 copy.85
  1.6 0.7 convert_element_type.5
  2.3 0.7 maximum_bitcast_fusion.1
  3.0 5.2 %all-to-all-start.1 = ((f32[4,2,17,128]{3,1,2,0:T(2,128)}), f32[4,2,17,128]{3,1,2,0:T(2,128)S(1)}, u32[]{:S(2)}, u32[]{:S(2)}) async-start(f32[4,2,17,128]{3,1,2,0:T(2,128)} %maximum_bitcast_fusion.1), calls=%async_computation.1 | async-start | bytes 139264 | tf_op jit(solution)/shard_map/all_to_all | solution.py:523
  8.2 3.1 %copy.79 = bf16[2,128,4096]{1,2,0:T(8,128)(2,1)S(1)} copy(bf16[2,128,4096]{2,1,0:T(8,128)(2,1)} %param.9) | data formatting | bytes 4194304 | tf_op args[0]
  11.3 4.1 %copy.80 = bf16[2,128,4096]{1,2,0:T(8,128)(2,1)} copy(bf16[2,128,4096]{2,1,0:T(8,128)(2,1)} %param.10) | data formatting | bytes 4194304 | tf_op args[1]
  15.4 0.2 copy.81
  15.6 0.2 copy.82
  15.7 1.7 maximum_bitcast_fusion
  17.5 2.5 %copy.83 = bf16[4,2,128,2304]{2,3,1,0:T(8,128)(2,1)} copy(bf16[4,2,128,2304]{2,3,0,1:T(8,128)(2,1)S(1)} %maximum_bitcast_fusion) | data formatting | bytes 9437184 | tf_op jit(solution)/shard_map/transpose | solution.py:529
  19.9 5.1 %all-to-all-start = ((bf16[4,2,128,2304]{2,3,1,0:T(8,128)(2,1)}), bf16[4,2,128,2304]{2,3,1,0:T(8,128)(2,1)}, u32[]{:S(2)}, u32[]{:S(2)}) async-start(bf16[4,2,128,2304]{2,3,1,0:T(8,128)(2,1)} %copy.83), calls=%async_computation | async-start | bytes 9437184 | tf_op jit(solution)/shard_map/all_to_all | solution.py:523
  25.7 0.1 dynamic_slice.6
  25.8 0.5 pad_bitcast_fusion.rate_ref
  26.3 0.6 constant_dynamic-slice_fusion.w_ref
  27.0 0.1 negate_multiply_fusion
  27.2 3.5 %collective-permute-start.1 = (f32[2,2]{1,0:T(2,128)S(1)}, f32[2,2]{1,0:T(2,128)S(1)}, u32[]{:S(2)}, u32[]{:S(2)}) collective-permute-start(f32[2,2]{1,0:T(2,128)S(1)} %slice.85), channel_id=1, source_target_pairs={{0,8},{8,16},{16,24},{1,9},{9,17},{17,25},{2,10},{10,18},{18,26},{... | collective-permute-start | bytes 56 | tf_op jit(solution)/shard_map/ppermute | solution.py:546
  30.7 0.3 fusion
  31.0 0.2 slice_reduce_fusion.2
  31.1 0.2 slice_reduce_fusion.1
  31.3 0.1 compare_convert_fusion
  31.4 0.1 slice_bitcast_fusion.1
  31.5 0.2 slice_reduce_fusion
  31.8 0.7 broadcast_in_dim_reshape.3.through_ref
  32.6 0.1 fusion.7
  32.8 0.3 concatenate.23.row_ref
  33.0 1.0 copy.104.tok_ref
  34.1 44.0 %all-to-all-done = bf16[4,2,128,2304]{2,3,1,0:T(8,128)(2,1)} async-done(((bf16[4,2,128,2304]{2,3,1,0:T(8,128)(2,1)}), bf16[4,2,128,2304]{2,3,1,0:T(8,128)(2,1)}, u32[]{:S(2)}, u32[]{:S(2)}) %all-to-all-start) | async-done | bytes 4718624 | tf_op jit(solution)/shard_map/all_to_all | solution.py:523
  78.1 2.8 %copy_bitcast_fusion = bf16[2,512,2304]{1,2,0:T(8,128)(2,1)S(1)} fusion(bf16[4,2,128,2304]{2,3,1,0:T(8,128)(2,1)} %all-to-all-done), kind=kLoop, calls=%fused_computation | loop fusion | bytes 9437184 | tf_op jit(solution)/shard_map/reshape | solution.py:530
  80.9 1.6 fusion.13
  82.5 1.1 slice.74
  83.6 3.5 %collective-permute-start = (bf16[2,16,1024]{1,2,0:T(8,128)(2,1)}, bf16[2,16,1024]{1,2,0:T(8,128)(2,1)S(1)}, u32[]{:S(2)}, u32[]{:S(2)}) collective-permute-start(bf16[2,16,1024]{1,2,0:T(8,128)(2,1)} %slice.74), channel_id=1, source_target_pairs={{0,8},{8,16},{16,24},{1,9},{9,17},{17,25},{2,10},{10,18},{18,26},{... | collective-permute-start | bytes 196616 | tf_op jit(solution)/shard_map/ppermute | solution.py:545
  87.1 0.9 slice_bitcast_fusion.3
  88.0 2.5 %copy.101.t_ref = bf16[2,512,1024]{2,1,0:T(8,128)(2,1)} copy(bf16[2,512,1024]{1,2,0:T(8,128)(2,1)S(1)} %get-tuple-element.27) | data formatting | bytes 4194304 | tf_op jit(solution)/shard_map/slice | solution.py:532
  90.5 0.8 copy.102.b_ref
  91.3 0.8 copy.103.c_ref
  92.1 5.6 %collective-permute-done = bf16[2,16,1024]{1,2,0:T(8,128)(2,1)S(1)} collective-permute-done((bf16[2,16,1024]{1,2,0:T(8,128)(2,1)}, bf16[2,16,1024]{1,2,0:T(8,128)(2,1)S(1)}, u32[]{:S(2)}, u32[]{:S(2)}) %collective-permute-start) | collective-permute-done | bytes 65568 | tf_op jit(solution)/shard_map/ppermute | solution.py:545
  97.8 3.0 %pad_maximum_fusion = bf16[2,528,1024]{1,2,0:T(8,128)(2,1)S(1)} fusion(bf16[2,512,1024]{1,2,0:T(8,128)(2,1)} %get-tuple-element.28, bf16[2,16,1024]{1,2,0:T(8,128)(2,1)S(1)} %collective-permute-done), kind=kLoop, calls=%fused_computation.2 | loop fusion | flops 4325376 | bytes 4325376 | tf_op jit(solution)/shard_map/concatenate | solution.py:547
  100.8 2.6 %copy.100.x_ref = bf16[2,528,1024]{2,1,0:T(8,128)(2,1)} copy(bf16[2,528,1024]{1,2,0:T(8,128)(2,1)S(1)} %pad_maximum_fusion) | data formatting | bytes 4325376 | tf_op jit(solution)/shard_map/concatenate | solution.py:547
  103.4 13.9 %ends.1 = (f32[2,128,1024]{2,1,0:T(8,128)}, f32[2,128,1024]{2,1,0:T(8,128)}) custom-call(bf16[2,528,1024]{2,1,0:T(8,128)(2,1)} %copy.100.x_ref, bf16[2,512,1024]{2,1,0:T(8,128)(2,1)} %copy.101.t_ref, bf16[2,128,512]{2,1,0:T(8,128)(2,1)} %get-tuple-element.24.bt_ref, bf16[2,128,512]{2,1,0:T(8,128)(2,1)} %get-tuple-element.23.ct_ref, ...), custom_call_target="tpu_custom_call" | custom-call | tf_op jit(solution)/shard_map/ends/pallas_call | solution.py:223
  117.3 45.8 %chain.1 = (f32[8,32,1024]{2,1,0:T(8,128)}, f32[8,32,1024]{2,1,0:T(8,128)}) custom-call(f32[2,1,1024]{2,1,0:T(1,128)} %broadcast_in_dim_reshape.3.through_ref, f32[8,32,1024]{2,1,0:T(8,128)} %bitcast.74, f32[8,32,1024]{2,1,0:T(8,128)} %bitcast.75), custom_call_target="tpu_custom_call" | custom-call | tf_op jit(solution)/shard_map/chain/pallas_call | solution.py:353
  163.1 35.0 %main.1 = (f32[2,528,1024]{2,1,0:T(8,128)}, f32[2,512,128]{2,1,0:T(8,128)}, f32[2,8,1024]{2,1,0:T(8,128)}) custom-call(bf16[2,528,1024]{2,1,0:T(8,128)(2,1)} %copy.100.x_ref, bf16[2,512,1024]{2,1,0:T(8,128)(2,1)} %copy.101.t_ref, bf16[2,512,128]{2,1,0:T(8,128)(2,1)} %copy.102.b_ref, bf16[2,512,128]{2,1,0:T(8,128)(2,1)} %copy.103.c_ref, ...), custom_call_target="tpu_custom_call" | custom-call | tf_op jit(solution)/shard_map/main/pallas_call | solution.py:242
  198.1 1.2 copy.105
  199.4 0.7 fusion.2.raw_ref
  200.0 0.7 broadcast_in_dim.57.sign_ref
  200.7 37.9 %finish.1 = (f32[8,128]{1,0:T(8,128)}, bf16[2,128,4096]{2,1,0:T(8,128)(2,1)}, f32[2,64,128]{2,1,0:T(8,128)}) custom-call(f32[2,528,1024]{2,1,0:T(8,128)} %get-tuple-element.17.grad_ref, f32[2,8,1024]{2,1,0:T(8,128)} %get-tuple-element.18.score_ref, f32[2,16,512]{2,1,0:T(8,128)} %fusion.2.raw_ref, f32[8,128]{1,0:T(8,128)} %broadcast_in_dim.57.sign_ref), custom_call_target="tpu_custom_call" | custom-call | tf_op jit(solution)/shard_map/finish/pallas_call | solution.py:479
  238.6 1.2 slice.73
  239.8 3.1 %copy.129 = bf16[2,128,4096]{2,1,0:T(8,128)(2,1)} copy(bf16[2,128,4096]{2,1,0:T(8,128)(2,1)} %get-tuple-element.47) | data formatting | bytes 4194304
  242.9 1.5 copy.130
  (32 shorter events, 0.5 us)
Async XLA Ops:
  0.6 25.7 %copy-start = (f32[4,4096]{1,0:T(4,128)S(1)}, f32[4,4096]{1,0:T(4,128)}, u32[]{:S(2)}) copy-start(f32[4,4096]{1,0:T(4,128)} %param.16) | copy-start | bytes 196612
  0.6 14.7 %copy-start.2 = (bf16[2,128,512]{2,1,0:T(8,128)(2,1)S(1)}, bf16[2,128,512]{2,1,0:T(8,128)(2,1)}, u32[]{:S(2)}) copy-start(bf16[2,128,512]{2,1,0:T(8,128)(2,1)} %param.11) | copy-start | bytes 786436
  0.7 14.9 %copy-start.3 = (bf16[2,128,512]{2,1,0:T(8,128)(2,1)S(1)}, bf16[2,128,512]{2,1,0:T(8,128)(2,1)}, u32[]{:S(2)}) copy-start(bf16[2,128,512]{2,1,0:T(8,128)(2,1)} %param.12) | copy-start | bytes 786436
  3.0 17.0 %all-to-all-start.1 = ((f32[4,2,17,128]{3,1,2,0:T(2,128)}), f32[4,2,17,128]{3,1,2,0:T(2,128)S(1)}, u32[]{:S(2)}, u32[]{:S(2)}) async-start(f32[4,2,17,128]{3,1,2,0:T(2,128)} %maximum_bitcast_fusion.1), calls=%async_computation.1 | async-start | bytes 139264 | tf_op jit(solution)/shard_map/all_to_all | solution.py:523
  19.9 5.8 %copy-start.4 = (f32[64]{0:T(128)S(1)}, f32[64]{0:T(128)}, u32[]{:S(2)}) copy-start(f32[64]{0:T(128)} %param.15) | copy-start | bytes 772
  19.9 58.1 %all-to-all-start = ((bf16[4,2,128,2304]{2,3,1,0:T(8,128)(2,1)}), bf16[4,2,128,2304]{2,3,1,0:T(8,128)(2,1)}, u32[]{:S(2)}, u32[]{:S(2)}) async-start(bf16[4,2,128,2304]{2,3,1,0:T(8,128)(2,1)} %copy.83), calls=%async_computation | async-start | bytes 9437184 | tf_op jit(solution)/shard_map/all_to_all | solution.py:523
  27.2 5.3 %collective-permute-start.1 = (f32[2,2]{1,0:T(2,128)S(1)}, f32[2,2]{1,0:T(2,128)S(1)}, u32[]{:S(2)}, u32[]{:S(2)}) collective-permute-start(f32[2,2]{1,0:T(2,128)S(1)} %slice.85), channel_id=1, source_target_pairs={{0,8},{8,16},{16,24},{1,9},{9,17},{17,25},{2,10},{10,18},{18,26},{... | collective-permute-start | bytes 56 | tf_op jit(solution)/shard_map/ppermute | solution.py:546
  33.0 47.9 %copy-start.1 = (f32[2,128,512]{2,1,0:T(8,128)}, f32[2,128,512]{2,1,0:T(8,128)S(1)}, u32[]{:S(2)}) copy-start(f32[2,128,512]{2,1,0:T(8,128)S(1)} %concatenate.23.row_ref) | copy-start | bytes 1572868
  83.6 14.2 %collective-permute-start = (bf16[2,16,1024]{1,2,0:T(8,128)(2,1)}, bf16[2,16,1024]{1,2,0:T(8,128)(2,1)S(1)}, u32[]{:S(2)}, u32[]{:S(2)}) collective-permute-start(bf16[2,16,1024]{1,2,0:T(8,128)(2,1)} %slice.74), channel_id=1, source_target_pairs={{0,8},{8,16},{16,24},{1,9},{9,17},{17,25},{2,10},{10,18},{18,26},{... | collective-permute-start | bytes 196616 | tf_op jit(solution)/shard_map/ppermute | solution.py:545
